TPU v7x, 256 devices: a whole 4x4x8 slice. The times are simulated.
256 devices in a mesh: replica: 8 (over x, core), mp: 32 (over y, z).
Axes of the slice: x: 4, y: 4, z: 8, core: 2. Of those that a mesh axis runs over, the one named last changes fastest.
Arguments:
- emb_table: float32 [131072, 256], P('mp'), may hold values from -3 to 3
- row_accum: float32 [131072], P('mp'), may hold values from 0.05 to 5
- row_grads: bfloat16 [1048576, 256], P(('replica', 'mp')), may hold values from -6 to 6
- owner_ids: int32 [1048576, 1], P(('replica', 'mp')), may hold values from 0 to 31; in each aligned block of 4096 rows (0 to 4095, 4096 to 8191, ...) at most 256 rows name the same one
- local_row: int32 [1048576], P(('replica', 'mp')), may hold values from 0 to 4095
Outputs:
- new_table: float32 [131072, 256], P('mp')
- new_accum: float32 [131072], P('mp')
Inputs may be any that keep to these rules, and one draw needn't show every extreme that they name: `owner_ids`: among the lookups of one device, no owner is named more than 256 times, a bound that some block reaches.
All inputs are finite; a program needn't handle non-finite values.
Results may differ from a plain program's by a relative error of at most 0.0003.
Values may be sent and summed in bfloat16 or wider, within the bound.
No kernel may reach another device: no remote copies, remote signals or barrier semaphores. Data moves between devices by JAX's collectives and lax.ppermute only.
A program may use at most 64 MiB of HBM per device.

v0:
```python
import jax
import jax.numpy as jnp
from jax import lax
from jax.sharding import PartitionSpec as P

learn_rate = 0.5


def shards(emb_table, row_accum, row_grads, owner_ids, local_row):
    owners_count = lax.axis_size("mp")
    replicas = lax.axis_size("replica")
    sample_count = row_grads.shape[0]
    feature_dim = row_grads.shape[1]
    local_rows = emb_table.shape[0]
    capacity = 2 * sample_count // owners_count
    dest_owner = owner_ids[:, 0]
    owner_hits = (dest_owner[:, None] == jnp.arange(owners_count, dtype=jnp.int32)[None, :]).astype(
        jnp.int32
    )
    position = jnp.sum((jnp.cumsum(owner_hits, axis=0) - 1) * owner_hits, axis=1)
    slot_index = dest_owner * capacity + position
    outgoing = (
        jnp.zeros((owners_count * capacity, feature_dim), jnp.bfloat16)
        .at[slot_index]
        .set(row_grads)
    )
    targets = jnp.full((owners_count * capacity,), -1, jnp.int32).at[slot_index].set(local_row)
    incoming, rows_in = (
        lax.all_to_all(
            outgoing.reshape(owners_count, capacity, feature_dim),
            "mp",
            split_axis=0,
            concat_axis=0,
            tiled=True,
        ),
        lax.all_to_all(
            targets.reshape(owners_count, capacity), "mp", split_axis=0, concat_axis=0, tiled=True
        ),
    )
    received = incoming.reshape(owners_count * capacity, feature_dim)
    rows_flat = rows_in.reshape(owners_count * capacity)
    safe_rows = jnp.where(rows_flat < 0, local_rows, rows_flat)
    summed = jax.ops.segment_sum(
        received.astype(jnp.float32), safe_rows, num_segments=local_rows + 1
    )[:local_rows]
    mean_square = jnp.mean(summed * summed, axis=1)
    row_delta = -learn_rate * summed / jnp.sqrt(row_accum + mean_square)[:, None]
    delta_total, square_total = lax.psum((row_delta, mean_square), "replica")
    return (emb_table + delta_total / replicas, row_accum + square_total / replicas)


def solution(mesh):
    return jax.shard_map(
        shards,
        mesh=mesh,
        in_specs=(
            P("mp", None),
            P("mp"),
            P(("replica", "mp"), None),
            P(("replica", "mp"), None),
            P(("replica", "mp")),
        ),
        out_specs=(P("mp", None), P("mp")),
        check_vma=False,
    )
```

profile of v0, /device:TPU:1, one launch (start us, length us, event | category | flops | bytes accessed | tf_op | source)
XLA Modules:
  0.0 347.2 jit_solution(8560061589567669764)
XLA Ops:
  7.2 0.8 fusion.7
  7.9 9.2 %reduce-window.6 = s32[32,32,128]{2,1,0:T(8,128)S(1)} reduce-window(s32[32,32,128]{2,1,0:T(8,128)S(1)} %fusion.7, s32[]{:T(128)} %constant.13.clone.1), window={size=1x1x128 pad=0_0x0_0x127_0}, to_apply=%region_0.0 | reduce-window | flops 16646144 | bytes 1048580 | tf_op jit(solution)/shard_map/reduce-window
  17.2 0.8 slice_reduce_fusion
  18.0 0.2 reduce-window.9
  18.1 0.2 add_add_fusion
  18.4 1.1 fusion.6
  19.4 0.7 compare_select_fusion.1
  20.2 16.3 %scatter_custom_fusion = s32[8192]{0:T(1024)} fusion(s32[4096]{0:T(1024)S(1)} %bitcast.32, s32[4096]{0:T(1024)} %param.9, s32[]{:T(128)} %constant.11.clone.1), kind=kCustom, calls=%fused_computation.23 | custom fusion | bytes 33280 | tf_op jit(solution)/shard_map/scatter | solution.py:27
  36.4 12.0 %all-to-all-start = ((s32[32,1,256]{2,1,0:T(1,128)}), s32[32,1,256]{2,1,0:T(1,128)S(1)}, u32[]{:S(2)}, u32[]{:S(2)}) async-start(s32[32,1,256]{2,1,0:T(1,128)} %bitcast.5), calls=%async_computation | async-start | bytes 65536 | tf_op jit(solution)/shard_map/all_to_all | solution.py:36
  48.5 20.9 %scatter_custom_fusion.1 = bf16[8192,256]{1,0:T(8,128)(2,1)} fusion(s32[4096]{0:T(1024)S(1)} %bitcast.33, bf16[4096,256]{1,0:T(8,128)(2,1)} %param.7, bf16[]{:T(256)} %constant.7.clone.1), kind=kCustom, calls=%fused_computation.9 | custom fusion | bytes 4194816 | tf_op jit(solution)/shard_map/scatter | solution.py:25
  69.4 0.0 all-to-all-done
  69.4 9.4 %all-to-all-start.1 = ((bf16[32,256,256]{2,1,0:T(8,128)(2,1)}), bf16[32,256,256]{2,1,0:T(8,128)(2,1)}, u32[]{:S(2)}, u32[]{:S(2)}) async-start(bf16[32,256,256]{2,1,0:T(8,128)(2,1)} %bitcast.24), calls=%async_computation.1 | async-start | bytes 8388608 | tf_op jit(solution)/shard_map/all_to_all | solution.py:29
  78.8 0.0 all-reduce.2.cloned.1.call-start
  78.9 94.9 %all-to-all-done.1 = bf16[32,256,256]{2,1,0:T(8,128)(2,1)} async-done(((bf16[32,256,256]{2,1,0:T(8,128)(2,1)}), bf16[32,256,256]{2,1,0:T(8,128)(2,1)}, u32[]{:S(2)}, u32[]{:S(2)}) %all-to-all-start.1) | async-done | bytes 4194336 | tf_op jit(solution)/shard_map/all_to_all | solution.py:29
  173.7 45.6 %scatter_custom_fusion.2 = f32[4097,256]{1,0:T(8,128)} fusion(s32[8192]{0:T(1024)S(1)} %bitcast.31, bf16[8192,256]{1,0:T(8,128)(2,1)} %bitcast.10, f32[]{:T(128)} %constant.10.clone.1), kind=kCustom, calls=%fused_computation.3 | custom fusion | flops 4194304 | bytes 8389636 | tf_op jit(solution)/shard_map/scatter-add | solution.py:43
  219.3 0.0 copy-start
  219.3 2.8 multiply_reduce_fusion
  222.1 22.8 %psum.15 = f32[4096]{0:T(1024)S(1)} all-reduce(f32[4096]{0:T(1024)S(1)} %broadcast_multiply_fusion), channel_id=1, replica_groups=mesh['replica'=8,'mp'=32] {'replica'}, use_global_device_ids=true, to_apply=%region_8.9 | all-reduce | flops 4096 | bytes 32768 | tf_op jit(solution)/shard_map/psum | solution.py:48
  244.9 0.0 copy-done
  244.9 0.6 multiply_add_fusion.1
  245.5 3.9 %multiply_divide_fusion = f32[4096,256]{1,0:T(8,128)} fusion(f32[4097,256]{1,0:T(8,128)} %scatter_custom_fusion.2, f32[4096]{0:T(1024)S(1)} %get-tuple-element.3), kind=kLoop, calls=%fused_computation.7 | loop fusion | flops 2097152 | bytes 8404992 | tf_op jit(solution)/shard_map/div | solution.py:47
  249.5 0.0 all-reduce.2.cloned.1.call-update
  249.5 84.8 %all-reduce.2.cloned.1.call-done = f32[4096,256]{1,0:T(8,128)} async-done(((f32[4096,256]{1,0:T(8,128)}), f32[4096,256]{1,0:T(8,128)}) %all-reduce.2.cloned.1.call-update) | async-done | bytes 4194320 | tf_op jit(solution)/shard_map/psum | solution.py:48
  334.3 6.0 %multiply_add_fusion = f32[4096,256]{1,0:T(8,128)} fusion(f32[4096,256]{1,0:T(8,128)} %param.5, f32[4096,256]{1,0:T(8,128)} %all-reduce.2.cloned.1.call-done), kind=kLoop, calls=%fused_computation.5 | loop fusion | flops 2097152 | bytes 12582912 | tf_op jit(solution)/shard_map/add | solution.py:49
  (2 shorter events, 0.0 us)
Async XLA Ops:
  36.4 33.0 %all-to-all-start = ((s32[32,1,256]{2,1,0:T(1,128)}), s32[32,1,256]{2,1,0:T(1,128)S(1)}, u32[]{:S(2)}, u32[]{:S(2)}) async-start(s32[32,1,256]{2,1,0:T(1,128)} %bitcast.5), calls=%async_computation | async-start | bytes 65536 | tf_op jit(solution)/shard_map/all_to_all | solution.py:36
  69.4 104.3 %all-to-all-start.1 = ((bf16[32,256,256]{2,1,0:T(8,128)(2,1)}), bf16[32,256,256]{2,1,0:T(8,128)(2,1)}, u32[]{:S(2)}, u32[]{:S(2)}) async-start(bf16[32,256,256]{2,1,0:T(8,128)(2,1)} %bitcast.24), calls=%async_computation.1 | async-start | bytes 8388608 | tf_op jit(solution)/shard_map/all_to_all | solution.py:29
  78.8 255.5 %all-reduce.2.cloned.1.call-start = ((), (), s32[]{:S(2)}) async-start(), calls=%async_computation.2 | async-start | bytes 8388608 | tf_op jit(solution)/shard_map/psum | solution.py:48
  219.3 25.6 %copy-start = (f32[4096]{0:T(1024)S(1)}, f32[4096]{0:T(1024)}, u32[]{:S(2)}) copy-start(f32[4096]{0:T(1024)} %param.6) | copy-start | bytes 49156
Sparse Core Ops, SparseCore 0:
  249.6 84.6 all-reduce.1
where the time goes:
time: 348 us; the launch traced here: 347 us
  waiting for transfers between devices  180 us (52%)
  other arithmetic  71.2 us (20%)
  local copies, waits for them, and re-layouts  38 us (11%)
  blocking collectives  22.8 us (7%)
  starting transfers between devices  21.4 us (6%)
  between operations  14.1 us (4%)
    all_to_all x1, waiting for transfers between devices, shards(): lax.all_to_all(outgoing.reshape(owners_count, capacity, feature_dim), 'mp...  94.9 us
    psum x1, waiting for transfers between devices, shards(): delta_total, square_total = lax.psum((row_delta, mean_square), 'replica')  84.8 us
    scatter-add x1, other arithmetic, shards(): jax.ops.segment_sum(received.astype(jnp.float32), safe_rows, num_segments...  45.6 us
    psum x1, blocking collectives, shards(): delta_total, square_total = lax.psum((row_delta, mean_square), 'replica')  22.8 us
    scatter x1, local copies, waits for them, and re-layouts, shards(): outgoing = jnp.zeros((owners_count * capacity, feature_dim), jnp.bfloat16...  20.9 us
    scatter x1, local copies, waits for them, and re-layouts, shards(): jnp.full((owners_count * capacity,), -1, jnp.int32).at[slot_index]  16.3 us
    all_to_all x1, starting transfers between devices, shards(): lax.all_to_all(targets.reshape(owners_count, capacity), 'mp', split_axis=...  12 us
    another operation x2, other arithmetic  9.41 us
  transfers between devices with their start and end apart: 3, of which 2 were waited for; matrix products, arithmetic and copies ran while one was open for 6% of the time, Pallas kernels for 0%

commit v1 on v0

v1 whole, which is shorter than its diff:
```python
import functools
import jax
import jax.numpy as jnp
from jax import lax
from jax.experimental import pallas as pl
from jax.experimental.pallas import tpu as pltpu
from jax.sharding import PartitionSpec as P

LANES = 128


def pack_kernel(owner_ref, row_ref, grads_ref, out_ref, x32, out32, slot_v, slot_s, sem, *, owners, cap, pad):
    nb = owner_ref.shape[0]
    n = nb * LANES
    sub = lax.broadcasted_iota(jnp.int32, (owners, LANES), 0)
    upper = (lax.broadcasted_iota(jnp.int32, (LANES, LANES), 0)
             < lax.broadcasted_iota(jnp.int32, (LANES, LANES), 1)).astype(jnp.bfloat16)
    cap_iota = lax.broadcasted_iota(jnp.int32, (cap, LANES), 0)
    carry = jnp.zeros((owners, 1), jnp.float32)
    tgt = jnp.zeros((2 * owners, cap), jnp.float32)
    for b in range(nb):
        own = owner_ref[b:b + 1, :]
        hit = sub == jnp.broadcast_to(own, (owners, LANES))
        hot = hit.astype(jnp.float32)
        before = jnp.dot(hot.astype(jnp.bfloat16), upper, preferred_element_type=jnp.float32)
        pos = jnp.sum(jnp.where(hit, before + carry, 0.0), axis=0, keepdims=True).astype(jnp.int32)
        carry = carry + jnp.sum(hot, axis=1, keepdims=True)
        slot_v[b:b + 1, :] = own * cap + pos
        code = row_ref[b:b + 1, :] + 1
        hi = (code >> 6).astype(jnp.float32)
        lo = (code & 63).astype(jnp.float32)
        lhs = jnp.concatenate([hot * hi, hot * lo], axis=0).astype(jnp.bfloat16)
        rhs = (cap_iota == jnp.broadcast_to(pos, (cap, LANES))).astype(jnp.float32).astype(jnp.bfloat16)
        tgt = tgt + lax.dot_general(lhs, rhs, (((1,), (1,)), ((), ())), preferred_element_type=jnp.float32)
    copy = pltpu.make_async_copy(slot_v, slot_s, sem)
    copy.start()
    tb = tgt.astype(jnp.bfloat16)
    parts = [tb[:owners, :LANES], tb[:owners, LANES:], tb[owners:, :LANES], tb[owners:, LANES:]]
    parts += [jnp.zeros((owners, LANES), jnp.bfloat16)] * (pad - 4)
    for k in range(pad):
        x = parts[k]
        for o in range(owners):
            out_ref[o, 2 * cap + k:2 * cap + k + 1, :] = x[o:o + 1, :]

    blk = 128

    @pl.loop(0, n // blk)
    def _(b):
        r = pl.multiple_of(b * blk, blk)
        g = grads_ref[pl.ds(r, blk), :].astype(jnp.float32)
        x32[pl.ds(2 * r, blk, stride=2), :] = g[:, :LANES]
        x32[pl.ds(2 * r + 1, blk, stride=2), :] = g[:, LANES:]

    copy.wait()

    @pl.loop(0, nb)
    def _(b):
        for j in range(LANES):
            s = slot_s[b, j]
            out32[pl.ds(2 * s, 2), :] = x32[pl.ds(2 * (b * LANES + j), 2), :]

    @pl.loop(0, owners)
    def _(o):
        out_ref[o, 0:2 * cap, :] = out32[pl.ds(pl.multiple_of(o * 2 * cap, 2 * cap), 2 * cap), :].astype(jnp.bfloat16)


def pack(owner, row, grads, owners, cap, pad=8):
    n = grads.shape[0]
    nb = n // LANES
    return pl.pallas_call(
        functools.partial(pack_kernel, owners=owners, cap=cap, pad=pad),
        out_shape=jax.ShapeDtypeStruct((owners, 2 * cap + pad, LANES), jnp.bfloat16),
        in_specs=[pl.BlockSpec(memory_space=pltpu.VMEM)] * 3,
        out_specs=pl.BlockSpec(memory_space=pltpu.VMEM),
        scratch_shapes=[
            pltpu.VMEM((2 * n, LANES), jnp.float32),
            pltpu.VMEM((2 * owners * cap, LANES), jnp.float32),
            pltpu.VMEM((nb, LANES), jnp.int32),
            pltpu.SMEM((nb, LANES), jnp.int32),
            pltpu.SemaphoreType.DMA,
        ],
        name="pack",
    )(owner, row, grads)


def reduce_kernel(recv_ref, acc_ref, delta_ref, ms_ref, xbuf, a0, a1, a2, a3, idx_v, idx_s, sem, *, cap, rows, lr):
    accs = [a0, a1, a2, a3]
    owners = recv_ref.shape[0]
    @pl.loop(0, owners)
    def _(o):
        t = recv_ref[o, 2 * cap:2 * cap + 8, :].astype(jnp.float32)
        code = (t[0:2] * 64.0 + t[2:4]).astype(jnp.int32)
        idx_v[pl.ds(2 * o, 2), :] = jnp.where(code == 0, 2 * rows, 2 * code - 2)
    copy = pltpu.make_async_copy(idx_v, idx_s, sem)
    copy.start()
    zb = 512
    @pl.loop(0, 2 * rows // zb)
    def _(b):
        for a in accs:
            a[pl.ds(pl.multiple_of(b * zb, zb), zb), :] = jnp.zeros((zb, LANES), jnp.float32)
    copy.wait()

    @pl.loop(0, owners)
    def _(o):
        xbuf[...] = recv_ref[o, 0:2 * cap, :].astype(jnp.float32)
        for h in range(2):
            @pl.loop(0, LANES // 16)
            def _(jb):
                for u in range(16):
                    j = jb * 16 + u
                    r = idx_s[2 * o + h, j]
                    a = accs[u % len(accs)]
                    a[pl.ds(r, 2), :] += xbuf[pl.ds(2 * (h * LANES + j), 2), :]

    rb = 128
    @pl.loop(0, rows // rb)
    def _(b):
        base = pl.multiple_of(b * 2 * rb, 2 * rb)
        lo = sum(a[pl.ds(base, rb, stride=2), :] for a in accs)
        hi = sum(a[pl.ds(base + 1, rb, stride=2), :] for a in accs)
        ms = (jnp.sum(lo * lo, axis=1, keepdims=True) + jnp.sum(hi * hi, axis=1, keepdims=True)) * (1.0 / 256.0)
        ms_b = jnp.broadcast_to(ms, (rb, LANES))
        acc_c = jnp.transpose(jnp.broadcast_to(acc_ref[pl.ds(b, 1), :], (rb, LANES)))
        coef = -lr / jnp.sqrt(acc_c + ms_b)
        r = pl.multiple_of(b * rb, rb)
        delta_ref[pl.ds(r, rb), 0:LANES] = lo * coef
        delta_ref[pl.ds(r, rb), LANES:2 * LANES] = hi * coef
        ms_ref[pl.ds(b, 1), :] = jnp.transpose(ms_b)[0:1, :]


def reduce(recv, acc2d, cap, lr):
    rows = acc2d.size
    return pl.pallas_call(
        functools.partial(reduce_kernel, cap=cap, rows=rows, lr=lr),
        out_shape=(jax.ShapeDtypeStruct((rows, 2 * LANES), jnp.float32),
                   jax.ShapeDtypeStruct(acc2d.shape, jnp.float32)),
        in_specs=[pl.BlockSpec(memory_space=pltpu.VMEM)] * 2,
        out_specs=(pl.BlockSpec(memory_space=pltpu.VMEM), pl.BlockSpec(memory_space=pltpu.VMEM)),
        scratch_shapes=[pltpu.VMEM((2 * cap, LANES), jnp.float32)]
        + [pltpu.VMEM((2 * rows + 8, LANES), jnp.float32)] * 4
        + [
            pltpu.VMEM((2 * recv.shape[0], LANES), jnp.int32),
            pltpu.SMEM((2 * recv.shape[0], LANES), jnp.int32),
            pltpu.SemaphoreType.DMA,
        ],
        name="reduce",
    )(recv, acc2d)


learn_rate = 0.5


def shards(emb_table, row_accum, row_grads, owner_ids, local_row):
    owners = lax.axis_size("mp")
    replicas = lax.axis_size("replica")
    n = row_grads.shape[0]
    rows = emb_table.shape[0]
    cap = 2 * n // owners
    own2d = owner_ids.reshape(n // LANES, LANES)
    row2d = local_row.reshape(n // LANES, LANES)
    outgoing = pack(own2d, row2d, row_grads, owners, cap)
    incoming = lax.all_to_all(outgoing, "mp", split_axis=0, concat_axis=0, tiled=True)
    delta, ms = reduce(incoming, row_accum.reshape(rows // LANES, LANES), cap, learn_rate)
    delta_total, square_total = lax.psum((delta, ms), "replica")
    return (emb_table + delta_total / replicas, row_accum + square_total.reshape(rows) / replicas)


def solution(mesh):
    return jax.shard_map(
        shards,
        mesh=mesh,
        in_specs=(
            P("mp", None),
            P("mp"),
            P(("replica", "mp"), None),
            P(("replica", "mp"), None),
            P(("replica", "mp")),
        ),
        out_specs=(P("mp", None), P("mp")),
        check_vma=False,
    )
```

time: 348 us -> 249 us (0.72)
  waiting for transfers between devices: 180 us -> 48.1 us
  blocking collectives: 22.8 us -> 133 us
  other arithmetic: 71.2 us -> 6.63 us
  Pallas kernels: 0 us -> 44.9 us
  local copies, waits for them, and re-layouts: 38 us -> 0.69 us
  starting transfers between devices: 21.4 us -> 0.04 us
    all_to_all x0 -> x1, blocking collectives: none -> 110 us  [shards(): lax.all_to_all(outgoing, 'mp', split_axis=0, concat_axis=0, tiled=True)]
    all_to_all x2 -> x0, waiting for transfers between devices: 94.9 us -> none  [the longest x1 94.9 us: shards(): lax.all_to_all(outgoing.reshape(owners_count, capacity, feature_dim), 'mp...]
    scatter-add x1 -> x0, other arithmetic: 45.6 us -> none  [shards(): jax.ops.segment_sum(received.astype(jnp.float32), safe_rows, num_segments...]
    pallas_call x0 -> x2, Pallas kernels: none -> 44.9 us  [the longest x1 33.3 us: reduce(): pl.pallas_call(functools.partial(reduce_kernel, cap=cap, rows=rows, lr=lr...]
    scatter x2 -> x0, local copies, waits for them, and re-layouts: 37.2 us -> none  [the longest x1 20.9 us: shards(): outgoing = jnp.zeros((owners_count * capacity, feature_dim), jnp.bfloat16...]
    psum x1, waiting for transfers between devices: 84.8 us -> 48.1 us  [shards(): delta_total, square_total = lax.psum((delta, ms), 'replica')]
    all_to_all x2 -> x0, starting transfers between devices: 21.4 us -> none  [the longest x1 12 us: shards(): lax.all_to_all(targets.reshape(owners_count, capacity), 'mp', split_axis=...]
    another operation x2 -> x0, other arithmetic: 9.41 us -> none
  transfers between devices with their start and end apart: 3 -> 1, of which waited for: 2 -> 1; matrix products, arithmetic and copies ran while one was open for 6% -> 0% of each run, Pallas kernels for 0% -> 0%
where the time goes in v1:
time: 249 us; the launch traced here: 247 us
  blocking collectives  133 us (53%)
  waiting for transfers between devices  48.1 us (19%)
  Pallas kernels  44.9 us (18%)
  between operations  14.1 us (6%)
  other arithmetic  6.63 us (3%)
    all_to_all x1, blocking collectives, shards(): lax.all_to_all(outgoing, 'mp', split_axis=0, concat_axis=0, tiled=True)  110 us
    psum x1, waiting for transfers between devices, shards(): delta_total, square_total = lax.psum((delta, ms), 'replica')  48.1 us
    pallas_call x1, Pallas kernels, reduce(): pl.pallas_call(functools.partial(reduce_kernel, cap=cap, rows=rows, lr=lr...  33.3 us
    psum x1, blocking collectives, shards(): delta_total, square_total = lax.psum((delta, ms), 'replica')  22.9 us
    pallas_call x1, Pallas kernels, pack(): pl.pallas_call(functools.partial(pack_kernel, owners=owners, cap=cap, pad...  11.5 us
    add x1, other arithmetic, shards(): emb_table + delta_total / replicas  6.02 us
  transfers between devices with their start and end apart: 1, of which 1 were waited for; matrix products, arithmetic and copies ran while one was open for 0% of the time, Pallas kernels for 0%

profile of v1, /device:TPU:1, one launch (start us, length us, event | category | flops | bytes accessed | tf_op | source)
XLA Modules:
  0.0 247.5 jit_solution(13619285573530106091)
XLA Ops:
  7.2 0.0 all-reduce.2.cloned.1.call-start
  7.2 11.5 %pack.1 = bf16[32,520,128]{2,1,0:T(8,128)(2,1)} custom-call(s32[32,128]{1,0:T(8,128)} %bitcast.6, s32[32,128]{1,0:T(8,128)} %bitcast.7, bf16[4096,256]{1,0:T(8,128)(2,1)} %grads_ref.1), custom_call_target="tpu_custom_call" | custom-call | tf_op jit(solution)/shard_map/pack/pallas_call | solution.py:70
  18.8 110.2 %all_to_all.5.recv_ref = bf16[32,520,128]{2,1,0:T(8,128)(2,1)} all-to-all(bf16[32,520,128]{2,1,0:T(8,128)(2,1)} %pack.1), channel_id=1, replica_groups=mesh['replica'=8,'mp'=32] {'mp'}, dimensions={0} | all-to-all | bytes 8519680 | tf_op jit(solution)/shard_map/all_to_all | solution.py:162
  128.9 0.0 copy-start
  128.9 33.3 %reduce.1 = (f32[4096,256]{1,0:T(8,128)}, f32[32,128]{1,0:T(8,128)}) custom-call(bf16[32,520,128]{2,1,0:T(8,128)(2,1)} %all_to_all.5.recv_ref, f32[32,128]{1,0:T(8,128)} %bitcast.5), custom_call_target="tpu_custom_call" | custom-call | tf_op jit(solution)/shard_map/reduce/pallas_call | solution.py:133
  162.3 0.0 copy-start.1
  162.3 0.0 all-reduce.2.cloned.1.call-update
  162.3 0.7 copy-done.1
  163.0 22.9 %psum.15 = f32[32,128]{1,0:T(8,128)S(1)} all-reduce(f32[32,128]{1,0:T(8,128)S(1)} %copy-done.1), channel_id=1, replica_groups=mesh['replica'=8,'mp'=32] {'replica'}, use_global_device_ids=true, to_apply=%region_1.0 | all-reduce | flops 4096 | bytes 32768 | tf_op jit(solution)/shard_map/psum | solution.py:164
  185.9 0.0 copy-done
  185.9 0.6 bitcast_add_fusion
  186.5 48.1 %all-reduce.2.cloned.1.call-done = f32[4096,256]{1,0:T(8,128)} async-done(((f32[4096,256]{1,0:T(8,128)}), f32[4096,256]{1,0:T(8,128)}) %all-reduce.2.cloned.1.call-update) | async-done | bytes 4194320 | tf_op jit(solution)/shard_map/psum | solution.py:164
  234.6 6.0 %multiply_add_fusion = f32[4096,256]{1,0:T(8,128)} fusion(f32[4096,256]{1,0:T(8,128)} %param.5, f32[4096,256]{1,0:T(8,128)} %all-reduce.2.cloned.1.call-done), kind=kLoop, calls=%fused_computation | loop fusion | flops 2097152 | bytes 12582912 | tf_op jit(solution)/shard_map/add | solution.py:165
Async XLA Ops:
  7.2 227.4 %all-reduce.2.cloned.1.call-start = ((), (), s32[]{:S(2)}) async-start(), calls=%async_computation.1 | async-start | bytes 8388608 | tf_op jit(solution)/shard_map/psum | solution.py:164
  128.9 57.0 %copy-start = (f32[4096]{0:T(1024)S(1)}, f32[4096]{0:T(1024)}, u32[]{:S(2)}) copy-start(f32[4096]{0:T(1024)} %param.6) | copy-start | bytes 49156
  162.3 0.7 copy-start.1
Sparse Core Ops, SparseCore 0:
  162.4 72.1 all-reduce.1

commit v2 on v1

--- a/solution.py
+++ b/solution.py
@@ -83,7 +83,7 @@
     )(owner, row, grads)
 
 
-def reduce_kernel(recv_ref, acc_ref, delta_ref, ms_ref, xbuf, a0, a1, a2, a3, idx_v, idx_s, sem, *, cap, rows, lr):
+def reduce_kernel(recv_ref, acc_ref, keep_ref, send_ref, xbuf, a0, a1, a2, a3, ms_v, idx_v, idx_s, sem, *, cap, rows, lr):
     accs = [a0, a1, a2, a3]
     owners = recv_ref.shape[0]
     @pl.loop(0, owners)
@@ -112,39 +112,209 @@
                     a = accs[u % len(accs)]
                     a[pl.ds(r, 2), :] += xbuf[pl.ds(2 * (h * LANES + j), 2), :]
 
-    rb = 128
-    @pl.loop(0, rows // rb)
-    def _(b):
-        base = pl.multiple_of(b * 2 * rb, 2 * rb)
-        lo = sum(a[pl.ds(base, rb, stride=2), :] for a in accs)
-        hi = sum(a[pl.ds(base + 1, rb, stride=2), :] for a in accs)
-        ms = (jnp.sum(lo * lo, axis=1, keepdims=True) + jnp.sum(hi * hi, axis=1, keepdims=True)) * (1.0 / 256.0)
-        ms_b = jnp.broadcast_to(ms, (rb, LANES))
-        acc_c = jnp.transpose(jnp.broadcast_to(acc_ref[pl.ds(b, 1), :], (rb, LANES)))
-        coef = -lr / jnp.sqrt(acc_c + ms_b)
-        r = pl.multiple_of(b * rb, rb)
-        delta_ref[pl.ds(r, rb), 0:LANES] = lo * coef
-        delta_ref[pl.ds(r, rb), LANES:2 * LANES] = hi * coef
-        ms_ref[pl.ds(b, 1), :] = jnp.transpose(ms_b)[0:1, :]
+    core = lax.rem(lax.axis_index("replica"), 2)
+    half = rows // 2
+    for ref, which in ((send_ref, 1 - core), (keep_ref, core)):
+
+        @pl.loop(0, half // LANES)
+        def _(b):
+            block = which * (half // LANES) + b
+            base = pl.multiple_of(block * 2 * LANES, 2 * LANES)
+            lo = sum(a[pl.ds(base, LANES, stride=2), :] for a in accs)
+            hi = sum(a[pl.ds(base + 1, LANES, stride=2), :] for a in accs)
+            ms = (jnp.sum(lo * lo, axis=1, keepdims=True) + jnp.sum(hi * hi, axis=1, keepdims=True)) * (
+                1.0 / (2 * LANES)
+            )
+            ms_b = jnp.broadcast_to(ms, (LANES, LANES))
+            acc_c = jnp.transpose(jnp.broadcast_to(acc_ref[pl.ds(block, 1), :], (LANES, LANES)))
+            coef = -lr / jnp.sqrt(acc_c + ms_b)
+            r = pl.multiple_of(b * LANES, LANES)
+            ref[pl.ds(r, LANES), 0:LANES] = lo * coef
+            ref[pl.ds(r, LANES), LANES : 2 * LANES] = hi * coef
+            ms_v[pl.ds(b, 1), :] = jnp.transpose(ms_b)[0:1, :]
+
+        ref[half : half + half // LANES, 0:LANES] = ms_v[...]
 
 
 def reduce(recv, acc2d, cap, lr):
     rows = acc2d.size
     return pl.pallas_call(
         functools.partial(reduce_kernel, cap=cap, rows=rows, lr=lr),
-        out_shape=(jax.ShapeDtypeStruct((rows, 2 * LANES), jnp.float32),
-                   jax.ShapeDtypeStruct(acc2d.shape, jnp.float32)),
+        out_shape=(jax.ShapeDtypeStruct((rows // 2 + rows // 2 // LANES, 2 * LANES), jnp.float32),) * 2,
         in_specs=[pl.BlockSpec(memory_space=pltpu.VMEM)] * 2,
         out_specs=(pl.BlockSpec(memory_space=pltpu.VMEM), pl.BlockSpec(memory_space=pltpu.VMEM)),
         scratch_shapes=[pltpu.VMEM((2 * cap, LANES), jnp.float32)]
         + [pltpu.VMEM((2 * rows + 8, LANES), jnp.float32)] * 4
         + [
+            pltpu.VMEM((rows // 2 // LANES, LANES), jnp.float32),
             pltpu.VMEM((2 * recv.shape[0], LANES), jnp.int32),
             pltpu.SMEM((2 * recv.shape[0], LANES), jnp.int32),
             pltpu.SemaphoreType.DMA,
         ],
         name="reduce",
     )(recv, acc2d)
+
+
+LOG_STEPS = 340.0
+FINE = 1.3e7
+FULL = 32767.0
+
+
+def put_log(x):
+    return jnp.floor(jnp.log(jnp.maximum(x, 1e-18)) * (LOG_STEPS / 0.6931471805599453))
+
+
+def get_log(code):
+    return jnp.exp(code * (0.6931471805599453 / LOG_STEPS))
+
+
+def put_pair(x):
+    hi = put_log(x)
+    lo = jnp.round((x / get_log(hi) - 1.0) * FINE)
+    return hi, jnp.clip(lo, -FULL, FULL)
+
+
+def get_pair(hi, lo):
+    return get_log(hi) * (1.0 + lo * (1.0 / FINE))
+
+
+def to_i16(x):
+    return x.astype(jnp.int32).astype(jnp.int16)
+
+
+def from_i16(x):
+    return x.astype(jnp.int32).astype(jnp.float32)
+
+
+def encode(ref, tail, j, t, ms_row):
+    top = jnp.max(jnp.abs(t), axis=1, keepdims=True)
+    top_b = jnp.broadcast_to(top, (LANES, LANES))
+    code = put_log(top_b) + 2.0
+    inv = FULL / get_log(code)
+    ref[j * LANES : (j + 1) * LANES, 0:LANES] = to_i16(jnp.clip(jnp.round(t[:, :LANES] * inv), -FULL, FULL))
+    ref[j * LANES : (j + 1) * LANES, LANES : 2 * LANES] = to_i16(
+        jnp.clip(jnp.round(t[:, LANES:] * inv), -FULL, FULL)
+    )
+    hi, lo = put_pair(ms_row)
+    tail[j : j + 1, 0:LANES] = jnp.transpose(code)[0:1, :]
+    tail[j : j + 1, LANES : 2 * LANES] = hi
+    tail[4 + j : 5 + j, 0:LANES] = lo
+
+
+def decode(ref, tail, j):
+    code = jnp.transpose(jnp.broadcast_to(tail[j : j + 1, 0:LANES], (LANES, LANES)))
+    step = get_log(code) * (1.0 / FULL)
+    lo = from_i16(ref[j * LANES : (j + 1) * LANES, 0:LANES]) * step
+    hi = from_i16(ref[j * LANES : (j + 1) * LANES, LANES : 2 * LANES]) * step
+    ms = get_pair(tail[j : j + 1, LANES : 2 * LANES], tail[4 + j : 5 + j, 0:LANES])
+    return lo, hi, ms
+
+
+def pair_kernel(keep_ref, recv_ref, own_ref, q1, q2, q3, tail, ms_v):
+    chip = lax.axis_index("replica") // 2
+    part = own_ref.shape[0] - 4
+    blocks = part // LANES
+    half = 4 * part
+    tail[...] = jnp.zeros_like(tail)
+    ms_at = slice(half, half + half // LANES)
+    ms_v[...] = keep_ref[ms_at, 0:LANES] + recv_ref[ms_at, 0:LANES]
+    for shift, ref in ((2, q2), (1, q1), (3, q3), (0, own_ref)):
+        quarter = lax.rem(chip + shift, 4)
+        for j in range(blocks):
+            b = quarter * blocks + j
+            r = pl.multiple_of(b * LANES, LANES)
+            t = keep_ref[pl.ds(r, LANES), :] + recv_ref[pl.ds(r, LANES), :]
+            ms = ms_v[pl.ds(b, 1), :]
+            if shift:
+                encode(ref, tail, j, t, ms)
+            else:
+                ref[j * LANES : (j + 1) * LANES, :] = t
+                ref[part + j : part + j + 1, 0:LANES] = ms
+        if shift:
+            ref[part : part + 16, :] = to_i16(tail[...])
+
+
+def pair_sum(keep, recv, part):
+    coded = jax.ShapeDtypeStruct((part + 16, 2 * LANES), jnp.int16)
+    return pl.pallas_call(
+        pair_kernel,
+        out_shape=(jax.ShapeDtypeStruct((part + 4, 2 * LANES), jnp.float32), coded, coded, coded),
+        in_specs=[pl.BlockSpec(memory_space=pltpu.VMEM)] * 2,
+        out_specs=(pl.BlockSpec(memory_space=pltpu.VMEM),) * 4,
+        scratch_shapes=[
+            pltpu.VMEM((16, 2 * LANES), jnp.float32),
+            pltpu.VMEM((4 * part // LANES, LANES), jnp.float32),
+        ],
+        name="pair_sum",
+    )(keep, recv)
+
+
+def chip_kernel(own_ref, r1, r2, r3, out_ref, tail, *, replicas):
+    part = own_ref.shape[0] - 4
+    tails = []
+    for k, ref in enumerate((r1, r2, r3)):
+        tail[16 * k : 16 * k + 16, :] = from_i16(ref[part : part + 16, :])
+        tails.append(tail.at[16 * k : 16 * k + 16, :])
+    last = tail.at[48:64, :]
+    last[...] = jnp.zeros_like(last)
+    for j in range(part // LANES):
+        lo = own_ref[j * LANES : (j + 1) * LANES, 0:LANES]
+        hi = own_ref[j * LANES : (j + 1) * LANES, LANES : 2 * LANES]
+        ms = own_ref[part + j : part + j + 1, 0:LANES]
+        for ref, t in zip((r1, r2, r3), tails):
+            lo_k, hi_k, ms_k = decode(ref, t, j)
+            lo, hi, ms = lo + lo_k, hi + hi_k, ms + ms_k
+        both = jnp.concatenate([lo, hi], axis=1) * (1.0 / replicas)
+        encode(out_ref, last, j, both, ms * (1.0 / replicas))
+    out_ref[part : part + 16, :] = to_i16(last[...])
+
+
+def chip_sum(own, r1, r2, r3, replicas):
+    return pl.pallas_call(
+        functools.partial(chip_kernel, replicas=replicas),
+        out_shape=jax.ShapeDtypeStruct(r1.shape, jnp.int16),
+        in_specs=[pl.BlockSpec(memory_space=pltpu.VMEM)] * 4,
+        out_specs=pl.BlockSpec(memory_space=pltpu.VMEM),
+        scratch_shapes=[pltpu.VMEM((64, 2 * LANES), jnp.float32)],
+        name="chip_sum",
+    )(own, r1, r2, r3)
+
+
+def update_kernel(order_ref, emb_ref, acc_ref, *refs):
+    pieces, (table_ref, accum_ref, tail) = refs[:-3], refs[-3:]
+    part = pieces[0].shape[0] - 16
+    blocks = part // LANES
+    step = pl.program_id(0)
+    for k, ref in enumerate(pieces):
+
+        @pl.when(step == k)
+        def _():
+            tail[...] = from_i16(ref[part : part + 16, :])
+            for j in range(blocks):
+                lo, hi, ms = decode(ref, tail, j)
+                rows = slice(j * LANES, (j + 1) * LANES)
+                table_ref[rows, 0:LANES] = emb_ref[rows, 0:LANES] + lo
+                table_ref[rows, LANES : 2 * LANES] = emb_ref[rows, LANES : 2 * LANES] + hi
+                at = pl.ds(order_ref[k] * blocks + j, 1)
+                accum_ref[at, :] = acc_ref[at, :] + ms
+
+
+def update(order, emb, acc2d, pieces):
+    part = pieces[0].shape[0] - 16
+    whole = lambda x: pl.BlockSpec(x.shape, lambda s, order: (0, 0))
+    moving = pl.BlockSpec((part, 2 * LANES), lambda s, order: (order[s], 0))
+    return pl.pallas_call(
+        update_kernel,
+        out_shape=(jax.ShapeDtypeStruct(emb.shape, jnp.float32), jax.ShapeDtypeStruct(acc2d.shape, jnp.float32)),
+        grid_spec=pltpu.PrefetchScalarGridSpec(
+            num_scalar_prefetch=1,
+            grid=(len(pieces),),
+            in_specs=[moving, whole(acc2d)] + [whole(p) for p in pieces],
+            out_specs=(moving, whole(acc2d)),
+            scratch_shapes=[pltpu.VMEM((16, 2 * LANES), jnp.float32)],
+        ),
+        name="update",
+    )(order, emb, acc2d, *pieces)
 
 
 learn_rate = 0.5
@@ -158,11 +328,28 @@
     cap = 2 * n // owners
     own2d = owner_ids.reshape(n // LANES, LANES)
     row2d = local_row.reshape(n // LANES, LANES)
+    acc2d = row_accum.reshape(rows // LANES, LANES)
     outgoing = pack(own2d, row2d, row_grads, owners, cap)
     incoming = lax.all_to_all(outgoing, "mp", split_axis=0, concat_axis=0, tiled=True)
-    delta, ms = reduce(incoming, row_accum.reshape(rows // LANES, LANES), cap, learn_rate)
-    delta_total, square_total = lax.psum((delta, ms), "replica")
-    return (emb_table + delta_total / replicas, row_accum + square_total.reshape(rows) / replicas)
+    keep, send = reduce(incoming, acc2d, cap, learn_rate)
+
+    def hop(v, chips):
+        return lax.ppermute(v, "replica", [(k, (k + 2 * chips) % replicas) for k in range(replicas)])
+
+    def swap(v):
+        return lax.ppermute(v, "replica", [(k, k ^ 1) for k in range(replicas)])
+
+    own, q1, q2, q3 = pair_sum(keep, swap(send), rows // replicas)
+    mine = chip_sum(own, hop(q1, 1), hop(q2, 2), hop(q3, 3), replicas)
+    here = [mine] + [hop(mine, s) for s in (1, 2, 3)]
+    there = [swap(v) for v in here]
+    me = lax.axis_index("replica")
+    chip, core = me // 2, me % 2
+    shift = jnp.arange(replicas // 2, dtype=jnp.int32)
+    quarter = (chip - shift) % 4
+    order = jnp.concatenate([core * 4 + quarter, (1 - core) * 4 + quarter]).astype(jnp.int32)
+    table, accum = update(order, emb_table, acc2d, here + there)
+    return table, accum.reshape(rows)
 
 
 def solution(mesh):

time: 249 us -> 217 us (0.87)
  blocking collectives: 133 us -> 110 us
  waiting for transfers between devices: 48.1 us -> 27.2 us
  Pallas kernels: 44.9 us -> 60.3 us
  starting transfers between devices: 0.04 us -> 14.3 us
  between operations: 14.1 us -> 0.7 us
  other arithmetic: 6.63 us -> 0.59 us
  local copies, waits for them, and re-layouts: 0.69 us -> 3.19 us
    psum x1 -> x0, waiting for transfers between devices: 48.1 us -> none  [shards(): delta_total, square_total = lax.psum((delta, ms), 'replica')]
    ppermute x0 -> x11, waiting for transfers between devices: none -> 27.2 us  [the longest x6 22.6 us: hop(): lax.ppermute(v, 'replica', [(k, (k + 2 * chips) % replicas) for k in rang...]
    psum x1 -> x0, blocking collectives: 22.9 us -> none  [shards(): delta_total, square_total = lax.psum((delta, ms), 'replica')]
    pallas_call x0 -> x3, Pallas kernels: none -> 15.4 us  [the longest x1 8.51 us: update(): pl.pallas_call(update_kernel, out_shape=(jax.ShapeDtypeStruct(emb.shape,...]
    ppermute x0 -> x11, starting transfers between devices: none -> 14.3 us  [the longest x6 8.02 us: hop(): lax.ppermute(v, 'replica', [(k, (k + 2 * chips) % replicas) for k in rang...]
    add x2 -> x1, other arithmetic: 6.63 us -> 0.01 us  [shards(): (1 - core) * 4 + quarter]
    unnamed x4 -> x22, local copies, waits for them, and re-layouts: 0.69 us -> 3.19 us
  transfers between devices with their start and end apart: 1 -> 11, of which waited for: 1 -> 6; matrix products, arithmetic and copies ran while one was open for 0% -> 0% of each run, Pallas kernels for 0% -> 0%
where the time goes in v2:
time: 217 us; the launch traced here: 216 us
  blocking collectives  110 us (51%)
  Pallas kernels  60.3 us (28%)
  waiting for transfers between devices  27.2 us (13%)
  starting transfers between devices  14.3 us (7%)
  local copies, waits for them, and re-layouts  3.19 us (1%)
    all_to_all x1, blocking collectives, shards(): lax.all_to_all(outgoing, 'mp', split_axis=0, concat_axis=0, tiled=True)  110 us
    pallas_call x1, Pallas kernels, reduce(): pl.pallas_call(functools.partial(reduce_kernel, cap=cap, rows=rows, lr=lr...  33.3 us
    ppermute x6, waiting for transfers between devices, hop(): lax.ppermute(v, 'replica', [(k, (k + 2 * chips) % replicas) for k in rang...  22.6 us
    pallas_call x1, Pallas kernels, pack(): pl.pallas_call(functools.partial(pack_kernel, owners=owners, cap=cap, pad...  11.6 us
    pallas_call x1, Pallas kernels, update(): pl.pallas_call(update_kernel, out_shape=(jax.ShapeDtypeStruct(emb.shape,...  8.51 us
    ppermute x6, starting transfers between devices, hop(): lax.ppermute(v, 'replica', [(k, (k + 2 * chips) % replicas) for k in rang...  8.02 us
    ppermute x5, starting transfers between devices, swap(): return lax.ppermute(v, 'replica', [(k, k ^ 1) for k in range(replicas)])  6.31 us
    ppermute x5, waiting for transfers between devices, swap(): return lax.ppermute(v, 'replica', [(k, k ^ 1) for k in range(replicas)])  4.57 us
  transfers between devices with their start and end apart: 11, of which 6 were waited for; matrix products, arithmetic and copies ran while one was open for 0% of the time, Pallas kernels for 0%

profile of v2, /device:TPU:1, one launch (start us, length us, event | category | flops | bytes accessed | tf_op | source)
XLA Modules:
  0.0 216.5 jit_solution(443624992696361024)
XLA Ops:
  0.6 11.6 %pack.1 = bf16[32,520,128]{2,1,0:T(8,128)(2,1)} custom-call(s32[32,128]{1,0:T(8,128)} %bitcast.6, s32[32,128]{1,0:T(8,128)} %bitcast.7, bf16[4096,256]{1,0:T(8,128)(2,1)} %grads_ref.1), custom_call_target="tpu_custom_call" | custom-call | tf_op jit(solution)/shard_map/pack/pallas_call | solution.py:70
  12.3 110.2 %all_to_all.5.recv_ref = bf16[32,520,128]{2,1,0:T(8,128)(2,1)} all-to-all(bf16[32,520,128]{2,1,0:T(8,128)(2,1)} %pack.1), channel_id=1, replica_groups=mesh['replica'=8,'mp'=32] {'mp'}, dimensions={0} | all-to-all | bytes 8519680 | tf_op jit(solution)/shard_map/all_to_all | solution.py:333
  122.4 33.3 %reduce.1 = (f32[2064,256]{1,0:T(8,128)}, f32[2064,256]{1,0:T(8,128)}) custom-call(bf16[32,520,128]{2,1,0:T(8,128)(2,1)} %all_to_all.5.recv_ref, f32[32,128]{1,0:T(8,128)} %bitcast.4), custom_call_target="tpu_custom_call" | custom-call | tf_op jit(solution)/shard_map/reduce/pallas_call | solution.py:141
  155.7 2.1 collective-permute-start
  157.8 4.0 %collective-permute-done.recv_ref = f32[2064,256]{1,0:T(8,128)S(1)} collective-permute-done((f32[2064,256]{1,0:T(8,128)}, f32[2064,256]{1,0:T(8,128)S(1)}, u32[]{:S(2)}, u32[]{:S(2)}) %collective-permute-start) | collective-permute-done | bytes 2113568 | tf_op jit(solution)/shard_map/ppermute | solution.py:340
  161.9 1.3 copy-done
  163.2 4.1 %pair_sum.1 = (f32[516,256]{1,0:T(8,128)}, s16[528,256]{1,0:T(8,128)(2,1)}, s16[528,256]{1,0:T(8,128)(2,1)}, s16[528,256]{1,0:T(8,128)(2,1)}) custom-call(f32[2064,256]{1,0:T(8,128)} %get-tuple-element.10.keep_ref, f32[2064,256]{1,0:T(8,128)} %copy-done), custom_call_target="tpu_custom_call" | custom-call | tf_op jit(solution)/shard_map/pair_sum/pallas_call | solution.py:239
  167.3 1.2 collective-permute-start.1
  168.5 2.5 %collective-permute-start.2 = (s16[528,256]{1,0:T(8,128)(2,1)}, s16[528,256]{1,0:T(8,128)(2,1)S(1)}, u32[]{:S(2)}, u32[]{:S(2)}) collective-permute-start(s16[528,256]{1,0:T(8,128)(2,1)} %get-tuple-element.14), channel_id=1, source_target_pairs={{0,128},{32,160},{64,192},{96,224},{128,0},{160,32},{192,64},{224,... | collective-permute-start | bytes 811016 | tf_op jit(solution)/shard_map/ppermute | solution.py:337
  171.0 1.1 collective-permute-start.3
  172.1 4.3 %collective-permute-done.1.r1 = s16[528,256]{1,0:T(8,128)(2,1)S(1)} collective-permute-done((s16[528,256]{1,0:T(8,128)(2,1)}, s16[528,256]{1,0:T(8,128)(2,1)S(1)}, u32[]{:S(2)}, u32[]{:S(2)}) %collective-permute-start.1) | collective-permute-done | bytes 270368 | tf_op jit(solution)/shard_map/ppermute | solution.py:337
  176.4 6.8 %collective-permute-done.2.r2 = s16[528,256]{1,0:T(8,128)(2,1)S(1)} collective-permute-done((s16[528,256]{1,0:T(8,128)(2,1)}, s16[528,256]{1,0:T(8,128)(2,1)S(1)}, u32[]{:S(2)}, u32[]{:S(2)}) %collective-permute-start.2) | collective-permute-done | bytes 270368 | tf_op jit(solution)/shard_map/ppermute | solution.py:337
  183.2 0.0 collective-permute-done.3.r3
  183.2 0.7 copy-done.9
  183.9 0.1 copy-done.10
  184.0 2.9 %chip_sum.1.refs_0_ = s16[528,256]{1,0:T(8,128)(2,1)} custom-call(f32[516,256]{1,0:T(8,128)} %get-tuple-element.12.own_ref, s16[528,256]{1,0:T(8,128)(2,1)} %copy-done.8, s16[528,256]{1,0:T(8,128)(2,1)} %copy-done.9, s16[528,256]{1,0:T(8,128)(2,1)} %copy-done.10), custom_call_target="tpu_custom_call" | custom-call | tf_op jit(solution)/shard_map/chip_sum/pallas_call | solution.py:273
  186.8 2.6 %collective-permute-start.6 = (s16[528,256]{1,0:T(8,128)(2,1)}, s16[528,256]{1,0:T(8,128)(2,1)S(1)}, u32[]{:S(2)}, u32[]{:S(2)}) collective-permute-start(s16[528,256]{1,0:T(8,128)(2,1)} %chip_sum.1.refs_0_), channel_id=1, source_target_pairs={{0,192},{32,224},{64,0},{96,32},{128,64},{160,96},{192,128},{224,1... | collective-permute-start | bytes 811016 | tf_op jit(solution)/shard_map/ppermute | solution.py:337
  189.4 0.2 collective-permute-start.5
  189.6 0.4 collective-permute-start.4
  190.0 2.0 collective-permute-start.7
  192.0 8.7 %collective-permute-done.6.refs_3_ = s16[528,256]{1,0:T(8,128)(2,1)S(1)} collective-permute-done((s16[528,256]{1,0:T(8,128)(2,1)}, s16[528,256]{1,0:T(8,128)(2,1)S(1)}, u32[]{:S(2)}, u32[]{:S(2)}) %collective-permute-start.6) | collective-permute-done | bytes 270368 | tf_op jit(solution)/shard_map/ppermute | solution.py:337
  200.8 1.5 collective-permute-start.10
  202.3 0.1 collective-permute-start.9
  202.4 2.8 %collective-permute-done.4.refs_1_ = s16[528,256]{1,0:T(8,128)(2,1)S(1)} collective-permute-done((s16[528,256]{1,0:T(8,128)(2,1)}, s16[528,256]{1,0:T(8,128)(2,1)S(1)}, u32[]{:S(2)}, u32[]{:S(2)}) %collective-permute-start.4) | collective-permute-done | bytes 270368 | tf_op jit(solution)/shard_map/ppermute | solution.py:337
  205.2 0.6 collective-permute-start.8
  205.8 0.6 pad_add_fusion.order_ref
  206.4 0.5 collective-permute-done.8.refs_5_
  206.9 0.1 copy-done.4
  207.1 0.1 copy-done.5
  207.2 0.1 copy-done.6
  207.3 0.7 copy-done.7
  208.0 8.5 %update.1 = (f32[4096,256]{1,0:T(8,128)}, f32[32,128]{1,0:T(8,128)}) custom-call(s32[8]{0:T(128)} %pad_add_fusion.order_ref, f32[4096,256]{1,0:T(8,128)} %emb_ref.1, f32[32,128]{1,0:T(8,128)} %bitcast.5, s16[528,256]{1,0:T(8,128)(2,1)} %chip_sum.1.refs_0_, s16[528,256]{1,0:T(8,128)(2,1)} %copy-done.3, s16[528,256]{1,0:T(8,128)(2,1)} %copy-done.2, ...), custom_call_target="tpu_custom_call" | custom-call | tf_op jit(solution)/shard_map/update/pallas_call | solution.py:306
  (20 shorter events, 0.0 us)
Async XLA Ops:
  155.7 6.1 %collective-permute-start = (f32[2064,256]{1,0:T(8,128)}, f32[2064,256]{1,0:T(8,128)S(1)}, u32[]{:S(2)}, u32[]{:S(2)}) collective-permute-start(f32[2064,256]{1,0:T(8,128)} %get-tuple-element.11), channel_id=1, source_target_pairs={{0,32},{32,0},{64,96},{96,64},{128,160},{160,128},{192,224},{224,1... | collective-permute-start | bytes 6340616 | tf_op jit(solution)/shard_map/ppermute | solution.py:340
  161.9 1.3 copy-start
  167.3 9.1 %collective-permute-start.1 = (s16[528,256]{1,0:T(8,128)(2,1)}, s16[528,256]{1,0:T(8,128)(2,1)S(1)}, u32[]{:S(2)}, u32[]{:S(2)}) collective-permute-start(s16[528,256]{1,0:T(8,128)(2,1)} %get-tuple-element.13), channel_id=1, source_target_pairs={{0,64},{32,96},{64,128},{96,160},{128,192},{160,224},{192,0},{224,... | collective-permute-start | bytes 811016 | tf_op jit(solution)/shard_map/ppermute | solution.py:337
  168.5 14.7 %collective-permute-start.2 = (s16[528,256]{1,0:T(8,128)(2,1)}, s16[528,256]{1,0:T(8,128)(2,1)S(1)}, u32[]{:S(2)}, u32[]{:S(2)}) collective-permute-start(s16[528,256]{1,0:T(8,128)(2,1)} %get-tuple-element.14), channel_id=1, source_target_pairs={{0,128},{32,160},{64,192},{96,224},{128,0},{160,32},{192,64},{224,... | collective-permute-start | bytes 811016 | tf_op jit(solution)/shard_map/ppermute | solution.py:337
  171.0 12.2 %collective-permute-start.3 = (s16[528,256]{1,0:T(8,128)(2,1)}, s16[528,256]{1,0:T(8,128)(2,1)S(1)}, u32[]{:S(2)}, u32[]{:S(2)}) collective-permute-start(s16[528,256]{1,0:T(8,128)(2,1)} %get-tuple-element.15), channel_id=1, source_target_pairs={{0,192},{32,224},{64,0},{96,32},{128,64},{160,96},{192,128},{224,1... | collective-permute-start | bytes 811016 | tf_op jit(solution)/shard_map/ppermute | solution.py:337
  176.4 6.8 %copy-start.8 = (s16[528,256]{1,0:T(8,128)(2,1)}, s16[528,256]{1,0:T(8,128)(2,1)S(1)}, u32[]{:S(2)}) copy-start(s16[528,256]{1,0:T(8,128)(2,1)S(1)} %collective-permute-done.1.r1) | copy-start | bytes 811012
  183.2 0.7 copy-start.9
  183.2 0.8 copy-start.10
  186.8 13.9 %collective-permute-start.6 = (s16[528,256]{1,0:T(8,128)(2,1)}, s16[528,256]{1,0:T(8,128)(2,1)S(1)}, u32[]{:S(2)}, u32[]{:S(2)}) collective-permute-start(s16[528,256]{1,0:T(8,128)(2,1)} %chip_sum.1.refs_0_), channel_id=1, source_target_pairs={{0,192},{32,224},{64,0},{96,32},{128,64},{160,96},{192,128},{224,1... | collective-permute-start | bytes 811016 | tf_op jit(solution)/shard_map/ppermute | solution.py:337
  189.4 12.8 %collective-permute-start.5 = (s16[528,256]{1,0:T(8,128)(2,1)}, s16[528,256]{1,0:T(8,128)(2,1)S(1)}, u32[]{:S(2)}, u32[]{:S(2)}) collective-permute-start(s16[528,256]{1,0:T(8,128)(2,1)} %chip_sum.1.refs_0_), channel_id=1, source_target_pairs={{0,128},{32,160},{64,192},{96,224},{128,0},{160,32},{192,64},{224,... | collective-permute-start | bytes 811016 | tf_op jit(solution)/shard_map/ppermute | solution.py:337
  189.6 15.5 %collective-permute-start.4 = (s16[528,256]{1,0:T(8,128)(2,1)}, s16[528,256]{1,0:T(8,128)(2,1)S(1)}, u32[]{:S(2)}, u32[]{:S(2)}) collective-permute-start(s16[528,256]{1,0:T(8,128)(2,1)} %chip_sum.1.refs_0_), channel_id=1, source_target_pairs={{0,64},{32,96},{64,128},{96,160},{128,192},{160,224},{192,0},{224,... | collective-permute-start | bytes 811016 | tf_op jit(solution)/shard_map/ppermute | solution.py:337
  190.0 16.3 %collective-permute-start.7 = (s16[528,256]{1,0:T(8,128)(2,1)}, s16[528,256]{1,0:T(8,128)(2,1)S(1)}, u32[]{:S(2)}, u32[]{:S(2)}) collective-permute-start(s16[528,256]{1,0:T(8,128)(2,1)} %chip_sum.1.refs_0_), channel_id=1, source_target_pairs={{0,32},{32,0},{64,96},{96,64},{128,160},{160,128},{192,224},{224,1... | collective-permute-start | bytes 811016 | tf_op jit(solution)/shard_map/ppermute | solution.py:340
  200.8 6.2 %copy-start.1 = (s16[528,256]{1,0:T(8,128)(2,1)}, s16[528,256]{1,0:T(8,128)(2,1)S(1)}, u32[]{:S(2)}) copy-start(s16[528,256]{1,0:T(8,128)(2,1)S(1)} %collective-permute-done.6.refs_3_) | copy-start | bytes 811012
  200.8 5.6 %collective-permute-start.10 = (s16[528,256]{1,0:T(8,128)(2,1)S(1)}, s16[528,256]{1,0:T(8,128)(2,1)S(1)}, u32[]{:S(2)}, u32[]{:S(2)}) collective-permute-start(s16[528,256]{1,0:T(8,128)(2,1)S(1)} %collective-permute-done.6.refs_3_), channel_id=1, source_target_pairs={{0,32},{32,0},{64,96},{96,64},{128,160},{160,128},{192,224},{224,1... | collective-permute-start | bytes 811016 | tf_op jit(solution)/shard_map/ppermute | solution.py:340
  202.3 4.7 %copy-start.2 = (s16[528,256]{1,0:T(8,128)(2,1)}, s16[528,256]{1,0:T(8,128)(2,1)S(1)}, u32[]{:S(2)}) copy-start(s16[528,256]{1,0:T(8,128)(2,1)S(1)} %collective-permute-done.5.refs_2_) | copy-start | bytes 811012
  202.3 4.1 %collective-permute-start.9 = (s16[528,256]{1,0:T(8,128)(2,1)S(1)}, s16[528,256]{1,0:T(8,128)(2,1)S(1)}, u32[]{:S(2)}, u32[]{:S(2)}) collective-permute-start(s16[528,256]{1,0:T(8,128)(2,1)S(1)} %collective-permute-done.5.refs_2_), channel_id=1, source_target_pairs={{0,32},{32,0},{64,96},{96,64},{128,160},{160,128},{192,224},{224,1... | collective-permute-start | bytes 811016 | tf_op jit(solution)/shard_map/ppermute | solution.py:340
  205.2 1.8 copy-start.3
  205.2 1.8 collective-permute-start.8
  206.4 0.7 copy-start.4
  206.4 0.8 copy-start.5
  206.4 0.9 copy-start.6
  207.3 0.7 copy-start.7

commit v3 on v2

--- a/solution.py
+++ b/solution.py
@@ -9,13 +9,23 @@
 LANES = 128
 
 
-def pack_kernel(owner_ref, row_ref, grads_ref, out_ref, x32, out32, slot_v, slot_s, sem, *, owners, cap, pad):
+def pack_kernel(
+    owner_hbm, row_hbm, grads_hbm, out_ref, owner_ref, row_ref, grads_ref, x32, out32, slot_v, slot_s, sems, *, owners, cap, pad
+):
+    loads = [
+        pltpu.make_async_copy(src, dst, sems.at[k])
+        for k, (src, dst) in enumerate(((owner_hbm, owner_ref), (row_hbm, row_ref), (grads_hbm, grads_ref)))
+    ]
+    for load in loads:
+        load.start()
     nb = owner_ref.shape[0]
     n = nb * LANES
     sub = lax.broadcasted_iota(jnp.int32, (owners, LANES), 0)
     upper = (lax.broadcasted_iota(jnp.int32, (LANES, LANES), 0)
              < lax.broadcasted_iota(jnp.int32, (LANES, LANES), 1)).astype(jnp.bfloat16)
     cap_iota = lax.broadcasted_iota(jnp.int32, (cap, LANES), 0)
+    loads[0].wait()
+    loads[1].wait()
     carry = jnp.zeros((owners, 1), jnp.float32)
     tgt = jnp.zeros((2 * owners, cap), jnp.float32)
     for b in range(nb):
@@ -25,14 +35,14 @@
         before = jnp.dot(hot.astype(jnp.bfloat16), upper, preferred_element_type=jnp.float32)
         pos = jnp.sum(jnp.where(hit, before + carry, 0.0), axis=0, keepdims=True).astype(jnp.int32)
         carry = carry + jnp.sum(hot, axis=1, keepdims=True)
-        slot_v[b:b + 1, :] = own * cap + pos
+        slot_v[b:b + 1, :] = 2 * (own * cap + pos)
         code = row_ref[b:b + 1, :] + 1
         hi = (code >> 6).astype(jnp.float32)
         lo = (code & 63).astype(jnp.float32)
         lhs = jnp.concatenate([hot * hi, hot * lo], axis=0).astype(jnp.bfloat16)
         rhs = (cap_iota == jnp.broadcast_to(pos, (cap, LANES))).astype(jnp.float32).astype(jnp.bfloat16)
         tgt = tgt + lax.dot_general(lhs, rhs, (((1,), (1,)), ((), ())), preferred_element_type=jnp.float32)
-    copy = pltpu.make_async_copy(slot_v, slot_s, sem)
+    copy = pltpu.make_async_copy(slot_v, slot_s, sems.at[3])
     copy.start()
     tb = tgt.astype(jnp.bfloat16)
     parts = [tb[:owners, :LANES], tb[:owners, LANES:], tb[owners:, :LANES], tb[owners:, LANES:]]
@@ -43,6 +53,7 @@
             out_ref[o, 2 * cap + k:2 * cap + k + 1, :] = x[o:o + 1, :]
 
     blk = 128
+    loads[2].wait()
 
     @pl.loop(0, n // blk)
     def _(b):
@@ -57,7 +68,7 @@
     def _(b):
         for j in range(LANES):
             s = slot_s[b, j]
-            out32[pl.ds(2 * s, 2), :] = x32[pl.ds(2 * (b * LANES + j), 2), :]
+            out32[pl.ds(s, 2), :] = x32[pl.ds(2 * (b * LANES + j), 2), :]
 
     @pl.loop(0, owners)
     def _(o):
@@ -70,17 +81,21 @@
     return pl.pallas_call(
         functools.partial(pack_kernel, owners=owners, cap=cap, pad=pad),
         out_shape=jax.ShapeDtypeStruct((owners, 2 * cap + pad, LANES), jnp.bfloat16),
-        in_specs=[pl.BlockSpec(memory_space=pltpu.VMEM)] * 3,
+        in_specs=[pl.BlockSpec(memory_space=pltpu.HBM)] * 3,
         out_specs=pl.BlockSpec(memory_space=pltpu.VMEM),
         scratch_shapes=[
+            pltpu.VMEM((nb, LANES), jnp.int32),
+            pltpu.VMEM((nb, LANES), jnp.int32),
+            pltpu.VMEM((n, 2 * LANES), jnp.bfloat16),
             pltpu.VMEM((2 * n, LANES), jnp.float32),
             pltpu.VMEM((2 * owners * cap, LANES), jnp.float32),
             pltpu.VMEM((nb, LANES), jnp.int32),
             pltpu.SMEM((nb, LANES), jnp.int32),
-            pltpu.SemaphoreType.DMA,
+            pltpu.SemaphoreType.DMA((4,)),
         ],
+        compiler_params=pltpu.CompilerParams(vmem_limit_bytes=24 << 20),
         name="pack",
-    )(owner, row, grads)
+    )(*[pltpu.with_memory_space_constraint(x, pltpu.HBM) for x in (owner, row, grads)])
 
 
 def reduce_kernel(recv_ref, acc_ref, keep_ref, send_ref, xbuf, a0, a1, a2, a3, ms_v, idx_v, idx_s, sem, *, cap, rows, lr):
@@ -104,13 +119,9 @@
     def _(o):
         xbuf[...] = recv_ref[o, 0:2 * cap, :].astype(jnp.float32)
         for h in range(2):
-            @pl.loop(0, LANES // 16)
-            def _(jb):
-                for u in range(16):
-                    j = jb * 16 + u
-                    r = idx_s[2 * o + h, j]
-                    a = accs[u % len(accs)]
-                    a[pl.ds(r, 2), :] += xbuf[pl.ds(2 * (h * LANES + j), 2), :]
+            for j in range(LANES):
+                at = pl.ds(idx_s[2 * o + h, j], 2)
+                accs[j % 4][at, :] += xbuf[2 * (h * LANES + j) : 2 * (h * LANES + j) + 2, :]
 
     core = lax.rem(lax.axis_index("replica"), 2)
     half = rows // 2
@@ -120,18 +131,18 @@
         def _(b):
             block = which * (half // LANES) + b
             base = pl.multiple_of(block * 2 * LANES, 2 * LANES)
-            lo = sum(a[pl.ds(base, LANES, stride=2), :] for a in accs)
-            hi = sum(a[pl.ds(base + 1, LANES, stride=2), :] for a in accs)
-            ms = (jnp.sum(lo * lo, axis=1, keepdims=True) + jnp.sum(hi * hi, axis=1, keepdims=True)) * (
-                1.0 / (2 * LANES)
-            )
-            ms_b = jnp.broadcast_to(ms, (LANES, LANES))
-            acc_c = jnp.transpose(jnp.broadcast_to(acc_ref[pl.ds(block, 1), :], (LANES, LANES)))
-            coef = -lr / jnp.sqrt(acc_c + ms_b)
+            lo, hi = [
+                (a0[at, :] + a1[at, :]) + (a2[at, :] + a3[at, :])
+                for at in (pl.ds(base, LANES, stride=2), pl.ds(base + 1, LANES, stride=2))
+            ]
+            total = jnp.sum(lo * lo + hi * hi, axis=1, keepdims=True)
+            ms = jnp.transpose(jnp.broadcast_to(total, (LANES, LANES)))[0:1, :] * (1.0 / (2 * LANES))
+            ms_v[pl.ds(b, 1), :] = ms
+            coef = -lr / jnp.sqrt(acc_ref[pl.ds(block, 1), :] + ms)
+            coef = jnp.transpose(jnp.broadcast_to(coef, (LANES, LANES)))
             r = pl.multiple_of(b * LANES, LANES)
             ref[pl.ds(r, LANES), 0:LANES] = lo * coef
             ref[pl.ds(r, LANES), LANES : 2 * LANES] = hi * coef
-            ms_v[pl.ds(b, 1), :] = jnp.transpose(ms_b)[0:1, :]
 
         ref[half : half + half // LANES, 0:LANES] = ms_v[...]
 
@@ -151,6 +162,7 @@
             pltpu.SMEM((2 * recv.shape[0], LANES), jnp.int32),
             pltpu.SemaphoreType.DMA,
         ],
+        compiler_params=pltpu.CompilerParams(vmem_limit_bytes=32 << 20),
         name="reduce",
     )(recv, acc2d)
 
@@ -245,6 +257,7 @@
             pltpu.VMEM((16, 2 * LANES), jnp.float32),
             pltpu.VMEM((4 * part // LANES, LANES), jnp.float32),
         ],
+        compiler_params=pltpu.CompilerParams(vmem_limit_bytes=12 << 20),
         name="pair_sum",
     )(keep, recv)
 
@@ -276,45 +289,58 @@
         in_specs=[pl.BlockSpec(memory_space=pltpu.VMEM)] * 4,
         out_specs=pl.BlockSpec(memory_space=pltpu.VMEM),
         scratch_shapes=[pltpu.VMEM((64, 2 * LANES), jnp.float32)],
+        compiler_params=pltpu.CompilerParams(vmem_limit_bytes=12 << 20),
         name="chip_sum",
     )(own, r1, r2, r3)
 
 
-def update_kernel(order_ref, emb_ref, acc_ref, *refs):
-    pieces, (table_ref, accum_ref, tail) = refs[:-3], refs[-3:]
-    part = pieces[0].shape[0] - 16
+def update_kernel(emb_hbm, acc_ref, *refs, pieces):
+    codes, (table_hbm, accum_ref, buf, tail, in_sems, out_sems) = refs[:pieces], refs[pieces:]
+    part = buf.shape[1]
     blocks = part // LANES
-    step = pl.program_id(0)
-    for k, ref in enumerate(pieces):
-
-        @pl.when(step == k)
-        def _():
-            tail[...] = from_i16(ref[part : part + 16, :])
-            for j in range(blocks):
-                lo, hi, ms = decode(ref, tail, j)
-                rows = slice(j * LANES, (j + 1) * LANES)
-                table_ref[rows, 0:LANES] = emb_ref[rows, 0:LANES] + lo
-                table_ref[rows, LANES : 2 * LANES] = emb_ref[rows, LANES : 2 * LANES] + hi
-                at = pl.ds(order_ref[k] * blocks + j, 1)
-                accum_ref[at, :] = acc_ref[at, :] + ms
-
-
-def update(order, emb, acc2d, pieces):
-    part = pieces[0].shape[0] - 16
-    whole = lambda x: pl.BlockSpec(x.shape, lambda s, order: (0, 0))
-    moving = pl.BlockSpec((part, 2 * LANES), lambda s, order: (order[s], 0))
-    return pl.pallas_call(
-        update_kernel,
+    me = lax.axis_index("replica")
+    chip, core = me // 2, lax.rem(me, 2)
+    places = [
+        (core if k < pieces // 2 else 1 - core) * (pieces // 2) + lax.rem(chip + pieces - k, pieces // 2)
+        for k in range(pieces)
+    ]
+    spans = [pl.ds(pl.multiple_of(place * part, part), part) for place in places]
+    loads = [pltpu.make_async_copy(emb_hbm.at[span], buf.at[k], in_sems.at[k]) for k, span in enumerate(spans)]
+    stores = [pltpu.make_async_copy(buf.at[k], table_hbm.at[span], out_sems.at[k]) for k, span in enumerate(spans)]
+    for load in loads:
+        load.start()
+    for k, ref in enumerate(codes):
+        tail[...] = from_i16(ref[part : part + 16, :])
+        loads[k].wait()
+        for j in range(blocks):
+            lo, hi, ms = decode(ref, tail, j)
+            rows = slice(j * LANES, (j + 1) * LANES)
+            buf[k, rows, 0:LANES] += lo
+            buf[k, rows, LANES : 2 * LANES] += hi
+            at = pl.ds(places[k] * blocks + j, 1)
+            accum_ref[at, :] = acc_ref[at, :] + ms
+        stores[k].start()
+    for store in stores:
+        store.wait()
+
+
+def update(emb, acc2d, codes):
+    part = codes[0].shape[0] - 16
+    pieces = len(codes)
+    return pl.pallas_call(
+        functools.partial(update_kernel, pieces=pieces),
         out_shape=(jax.ShapeDtypeStruct(emb.shape, jnp.float32), jax.ShapeDtypeStruct(acc2d.shape, jnp.float32)),
-        grid_spec=pltpu.PrefetchScalarGridSpec(
-            num_scalar_prefetch=1,
-            grid=(len(pieces),),
-            in_specs=[moving, whole(acc2d)] + [whole(p) for p in pieces],
-            out_specs=(moving, whole(acc2d)),
-            scratch_shapes=[pltpu.VMEM((16, 2 * LANES), jnp.float32)],
-        ),
+        in_specs=[pl.BlockSpec(memory_space=pltpu.HBM)] + [pl.BlockSpec(memory_space=pltpu.VMEM)] * (1 + pieces),
+        out_specs=(pl.BlockSpec(memory_space=pltpu.HBM), pl.BlockSpec(memory_space=pltpu.VMEM)),
+        scratch_shapes=[
+            pltpu.VMEM((pieces, part, 2 * LANES), jnp.float32),
+            pltpu.VMEM((16, 2 * LANES), jnp.float32),
+            pltpu.SemaphoreType.DMA((pieces,)),
+            pltpu.SemaphoreType.DMA((pieces,)),
+        ],
+        compiler_params=pltpu.CompilerParams(vmem_limit_bytes=20 << 20),
         name="update",
-    )(order, emb, acc2d, *pieces)
+    )(pltpu.with_memory_space_constraint(emb, pltpu.HBM), acc2d, *codes)
 
 
 learn_rate = 0.5
@@ -343,12 +369,7 @@
     mine = chip_sum(own, hop(q1, 1), hop(q2, 2), hop(q3, 3), replicas)
     here = [mine] + [hop(mine, s) for s in (1, 2, 3)]
     there = [swap(v) for v in here]
-    me = lax.axis_index("replica")
-    chip, core = me // 2, me % 2
-    shift = jnp.arange(replicas // 2, dtype=jnp.int32)
-    quarter = (chip - shift) % 4
-    order = jnp.concatenate([core * 4 + quarter, (1 - core) * 4 + quarter]).astype(jnp.int32)
-    table, accum = update(order, emb_table, acc2d, here + there)
+    table, accum = update(emb_table, acc2d, here + there)
     return table, accum.reshape(rows)
 
 

time: 217 us -> 189 us (0.87)
  Pallas kernels: 60.3 us -> 34.2 us
  local copies, waits for them, and re-layouts: 3.19 us -> 0.01 us
    pallas_call x1, Pallas kernels: 33.3 us -> 21 us  [reduce(): pl.pallas_call(functools.partial(reduce_kernel, cap=cap, rows=rows, lr=lr...]
    pallas_call x1, Pallas kernels: 8.51 us -> 3.95 us  [update(): pl.pallas_call(functools.partial(update_kernel, pieces=pieces), out_shape...]
    pallas_call x1, Pallas kernels: 11.6 us -> 7.58 us  [pack(): pl.pallas_call(functools.partial(pack_kernel, owners=owners, cap=cap, pad...]
    pallas_call x1, Pallas kernels: 4.08 us -> 0.78 us  [pair_sum(): pl.pallas_call(pair_kernel, out_shape=(jax.ShapeDtypeStruct((part + 4, 2...]
    unnamed x22 -> x2, local copies, waits for them, and re-layouts: 3.19 us -> 0.01 us
where the time goes in v3:
time: 189 us; the launch traced here: 187 us
  blocking collectives  110 us (58%)
  Pallas kernels  34.2 us (18%)
  waiting for transfers between devices  27.3 us (14%)
  starting transfers between devices  14.5 us (8%)
    all_to_all x1, blocking collectives, shards(): lax.all_to_all(outgoing, 'mp', split_axis=0, concat_axis=0, tiled=True)  110 us
    ppermute x6, waiting for transfers between devices, hop(): lax.ppermute(v, 'replica', [(k, (k + 2 * chips) % replicas) for k in rang...  22.3 us
    pallas_call x1, Pallas kernels, reduce(): pl.pallas_call(functools.partial(reduce_kernel, cap=cap, rows=rows, lr=lr...  21 us
    ppermute x6, starting transfers between devices, hop(): lax.ppermute(v, 'replica', [(k, (k + 2 * chips) % replicas) for k in rang...  8.31 us
    pallas_call x1, Pallas kernels, pack(): pl.pallas_call(functools.partial(pack_kernel, owners=owners, cap=cap, pad...  7.58 us
    ppermute x5, starting transfers between devices, swap(): return lax.ppermute(v, 'replica', [(k, k ^ 1) for k in range(replicas)])  6.23 us
    ppermute x5, waiting for transfers between devices, swap(): return lax.ppermute(v, 'replica', [(k, k ^ 1) for k in range(replicas)])  4.98 us
    pallas_call x1, Pallas kernels, update(): pl.pallas_call(functools.partial(update_kernel, pieces=pieces), out_shape...  3.95 us
  transfers between devices with their start and end apart: 11, of which 6 were waited for; matrix products, arithmetic and copies ran while one was open for 0% of the time, Pallas kernels for 0%

profile of v3, /device:TPU:1, one launch (start us, length us, event | category | flops | bytes accessed | tf_op | source)
XLA Modules:
  0.0 186.5 jit_solution(13048785113252193109)
XLA Ops:
  0.6 7.6 %pack.1 = bf16[32,520,128]{2,1,0:T(8,128)(2,1)S(1)} custom-call(s32[32,128]{1,0:T(8,128)} %bitcast.6, s32[32,128]{1,0:T(8,128)} %bitcast.7, bf16[4096,256]{1,0:T(8,128)(2,1)} %grads_hbm.1), custom_call_target="tpu_custom_call" | custom-call | tf_op jit(solution)/shard_map/pack/pallas_call | solution.py:81
  8.2 0.0 copy-start
  8.2 109.8 %all_to_all.5.recv_ref = bf16[32,520,128]{2,1,0:T(8,128)(2,1)S(1)} all-to-all(bf16[32,520,128]{2,1,0:T(8,128)(2,1)S(1)} %pack.1), channel_id=1, replica_groups=mesh['replica'=8,'mp'=32] {'mp'}, dimensions={0} | all-to-all | bytes 8519680 | tf_op jit(solution)/shard_map/all_to_all | solution.py:359
  118.0 0.0 copy-done
  118.0 21.0 %reduce.1 = (f32[2064,256]{1,0:T(8,128)S(1)}, f32[2064,256]{1,0:T(8,128)S(1)}) custom-call(bf16[32,520,128]{2,1,0:T(8,128)(2,1)S(1)} %all_to_all.5.recv_ref, f32[32,128]{1,0:T(8,128)S(1)} %bitcast.4), custom_call_target="tpu_custom_call" | custom-call | tf_op jit(solution)/shard_map/reduce/pallas_call | solution.py:152
  139.1 2.2 %collective-permute-start = (f32[2064,256]{1,0:T(8,128)S(1)}, f32[2064,256]{1,0:T(8,128)S(1)}, u32[]{:S(2)}, u32[]{:S(2)}) collective-permute-start(f32[2064,256]{1,0:T(8,128)S(1)} %get-tuple-element.11), channel_id=1, source_target_pairs={{0,32},{32,0},{64,96},{96,64},{128,160},{160,128},{192,224},{224,1... | collective-permute-start | bytes 6340616 | tf_op jit(solution)/shard_map/ppermute | solution.py:366
  141.3 3.8 %collective-permute-done.recv_ref = f32[2064,256]{1,0:T(8,128)S(1)} collective-permute-done((f32[2064,256]{1,0:T(8,128)S(1)}, f32[2064,256]{1,0:T(8,128)S(1)}, u32[]{:S(2)}, u32[]{:S(2)}) %collective-permute-start) | collective-permute-done | bytes 2113568 | tf_op jit(solution)/shard_map/ppermute | solution.py:366
  145.1 0.8 pair_sum.1
  145.9 1.2 collective-permute-start.1
  147.1 2.5 %collective-permute-start.2 = (s16[528,256]{1,0:T(8,128)(2,1)S(1)}, s16[528,256]{1,0:T(8,128)(2,1)S(1)}, u32[]{:S(2)}, u32[]{:S(2)}) collective-permute-start(s16[528,256]{1,0:T(8,128)(2,1)S(1)} %get-tuple-element.14), channel_id=1, source_target_pairs={{0,128},{32,160},{64,192},{96,224},{128,0},{160,32},{192,64},{224,... | collective-permute-start | bytes 811016 | tf_op jit(solution)/shard_map/ppermute | solution.py:363
  149.7 1.1 collective-permute-start.3
  150.8 4.1 %collective-permute-done.1.r1 = s16[528,256]{1,0:T(8,128)(2,1)S(1)} collective-permute-done((s16[528,256]{1,0:T(8,128)(2,1)S(1)}, s16[528,256]{1,0:T(8,128)(2,1)S(1)}, u32[]{:S(2)}, u32[]{:S(2)}) %collective-permute-start.1) | collective-permute-done | bytes 270368 | tf_op jit(solution)/shard_map/ppermute | solution.py:363
  154.9 6.8 %collective-permute-done.2.r2 = s16[528,256]{1,0:T(8,128)(2,1)S(1)} collective-permute-done((s16[528,256]{1,0:T(8,128)(2,1)S(1)}, s16[528,256]{1,0:T(8,128)(2,1)S(1)}, u32[]{:S(2)}, u32[]{:S(2)}) %collective-permute-start.2) | collective-permute-done | bytes 270368 | tf_op jit(solution)/shard_map/ppermute | solution.py:363
  161.7 0.0 collective-permute-done.3.r3
  161.7 0.9 chip_sum.1.refs_0_
  162.5 2.8 %collective-permute-start.6 = (s16[528,256]{1,0:T(8,128)(2,1)S(1)}, s16[528,256]{1,0:T(8,128)(2,1)S(1)}, u32[]{:S(2)}, u32[]{:S(2)}) collective-permute-start(s16[528,256]{1,0:T(8,128)(2,1)S(1)} %chip_sum.1.refs_0_), channel_id=1, source_target_pairs={{0,192},{32,224},{64,0},{96,32},{128,64},{160,96},{192,128},{224,1... | collective-permute-start | bytes 811016 | tf_op jit(solution)/shard_map/ppermute | solution.py:363
  165.3 0.2 collective-permute-start.5
  165.5 0.5 collective-permute-start.4
  166.0 1.9 %collective-permute-start.7 = (s16[528,256]{1,0:T(8,128)(2,1)S(1)}, s16[528,256]{1,0:T(8,128)(2,1)S(1)}, u32[]{:S(2)}, u32[]{:S(2)}) collective-permute-start(s16[528,256]{1,0:T(8,128)(2,1)S(1)} %chip_sum.1.refs_0_), channel_id=1, source_target_pairs={{0,32},{32,0},{64,96},{96,64},{128,160},{160,128},{192,224},{224,1... | collective-permute-start | bytes 811016 | tf_op jit(solution)/shard_map/ppermute | solution.py:366
  167.9 8.4 %collective-permute-done.6.refs_3_ = s16[528,256]{1,0:T(8,128)(2,1)S(1)} collective-permute-done((s16[528,256]{1,0:T(8,128)(2,1)S(1)}, s16[528,256]{1,0:T(8,128)(2,1)S(1)}, u32[]{:S(2)}, u32[]{:S(2)}) %collective-permute-start.6) | collective-permute-done | bytes 270368 | tf_op jit(solution)/shard_map/ppermute | solution.py:363
  176.3 1.5 collective-permute-start.10
  177.8 0.0 collective-permute-done.5.refs_2_
  177.8 0.0 collective-permute-start.9
  177.8 3.0 %collective-permute-done.4.refs_1_ = s16[528,256]{1,0:T(8,128)(2,1)S(1)} collective-permute-done((s16[528,256]{1,0:T(8,128)(2,1)S(1)}, s16[528,256]{1,0:T(8,128)(2,1)S(1)}, u32[]{:S(2)}, u32[]{:S(2)}) %collective-permute-start.4) | collective-permute-done | bytes 270368 | tf_op jit(solution)/shard_map/ppermute | solution.py:363
  180.8 0.6 collective-permute-start.8
  181.4 0.0 collective-permute-done.7.refs_4_
  181.4 0.0 collective-permute-done.10.refs_7_
  181.4 0.0 collective-permute-done.9.refs_6_
  181.4 1.2 collective-permute-done.8.refs_5_
  182.6 4.0 %update.1 = (f32[4096,256]{1,0:T(8,128)}, f32[32,128]{1,0:T(8,128)}) custom-call(f32[4096,256]{1,0:T(8,128)} %emb_hbm.1, f32[32,128]{1,0:T(8,128)S(1)} %bitcast.5, s16[528,256]{1,0:T(8,128)(2,1)S(1)} %chip_sum.1.refs_0_, s16[528,256]{1,0:T(8,128)(2,1)S(1)} %collective-permute-done.4.refs_1_, s16[528,256]{1,0:T(8,128)(2,1)S(1)} %collective-permute-done.5.refs_2_, ...), custom_call_target="tpu_custom_call" | custom-call | tf_op jit(solution)/shard_map/update/pallas_call | solution.py:330
Async XLA Ops:
  8.2 109.8 %copy-start = (f32[4096]{0:T(1024)S(1)}, f32[4096]{0:T(1024)}, u32[]{:S(2)}) copy-start(f32[4096]{0:T(1024)} %param.6) | copy-start | bytes 49156
  139.1 6.1 %collective-permute-start = (f32[2064,256]{1,0:T(8,128)S(1)}, f32[2064,256]{1,0:T(8,128)S(1)}, u32[]{:S(2)}, u32[]{:S(2)}) collective-permute-start(f32[2064,256]{1,0:T(8,128)S(1)} %get-tuple-element.11), channel_id=1, source_target_pairs={{0,32},{32,0},{64,96},{96,64},{128,160},{160,128},{192,224},{224,1... | collective-permute-start | bytes 6340616 | tf_op jit(solution)/shard_map/ppermute | solution.py:366
  145.9 8.9 %collective-permute-start.1 = (s16[528,256]{1,0:T(8,128)(2,1)S(1)}, s16[528,256]{1,0:T(8,128)(2,1)S(1)}, u32[]{:S(2)}, u32[]{:S(2)}) collective-permute-start(s16[528,256]{1,0:T(8,128)(2,1)S(1)} %get-tuple-element.13), channel_id=1, source_target_pairs={{0,64},{32,96},{64,128},{96,160},{128,192},{160,224},{192,0},{224,... | collective-permute-start | bytes 811016 | tf_op jit(solution)/shard_map/ppermute | solution.py:363
  147.1 14.5 %collective-permute-start.2 = (s16[528,256]{1,0:T(8,128)(2,1)S(1)}, s16[528,256]{1,0:T(8,128)(2,1)S(1)}, u32[]{:S(2)}, u32[]{:S(2)}) collective-permute-start(s16[528,256]{1,0:T(8,128)(2,1)S(1)} %get-tuple-element.14), channel_id=1, source_target_pairs={{0,128},{32,160},{64,192},{96,224},{128,0},{160,32},{192,64},{224,... | collective-permute-start | bytes 811016 | tf_op jit(solution)/shard_map/ppermute | solution.py:363
  149.7 12.0 %collective-permute-start.3 = (s16[528,256]{1,0:T(8,128)(2,1)S(1)}, s16[528,256]{1,0:T(8,128)(2,1)S(1)}, u32[]{:S(2)}, u32[]{:S(2)}) collective-permute-start(s16[528,256]{1,0:T(8,128)(2,1)S(1)} %get-tuple-element.15), channel_id=1, source_target_pairs={{0,192},{32,224},{64,0},{96,32},{128,64},{160,96},{192,128},{224,1... | collective-permute-start | bytes 811016 | tf_op jit(solution)/shard_map/ppermute | solution.py:363
  162.5 13.8 %collective-permute-start.6 = (s16[528,256]{1,0:T(8,128)(2,1)S(1)}, s16[528,256]{1,0:T(8,128)(2,1)S(1)}, u32[]{:S(2)}, u32[]{:S(2)}) collective-permute-start(s16[528,256]{1,0:T(8,128)(2,1)S(1)} %chip_sum.1.refs_0_), channel_id=1, source_target_pairs={{0,192},{32,224},{64,0},{96,32},{128,64},{160,96},{192,128},{224,1... | collective-permute-start | bytes 811016 | tf_op jit(solution)/shard_map/ppermute | solution.py:363
  165.3 12.5 %collective-permute-start.5 = (s16[528,256]{1,0:T(8,128)(2,1)S(1)}, s16[528,256]{1,0:T(8,128)(2,1)S(1)}, u32[]{:S(2)}, u32[]{:S(2)}) collective-permute-start(s16[528,256]{1,0:T(8,128)(2,1)S(1)} %chip_sum.1.refs_0_), channel_id=1, source_target_pairs={{0,128},{32,160},{64,192},{96,224},{128,0},{160,32},{192,64},{224,... | collective-permute-start | bytes 811016 | tf_op jit(solution)/shard_map/ppermute | solution.py:363
  165.5 15.3 %collective-permute-start.4 = (s16[528,256]{1,0:T(8,128)(2,1)S(1)}, s16[528,256]{1,0:T(8,128)(2,1)S(1)}, u32[]{:S(2)}, u32[]{:S(2)}) collective-permute-start(s16[528,256]{1,0:T(8,128)(2,1)S(1)} %chip_sum.1.refs_0_), channel_id=1, source_target_pairs={{0,64},{32,96},{64,128},{96,160},{128,192},{160,224},{192,0},{224,... | collective-permute-start | bytes 811016 | tf_op jit(solution)/shard_map/ppermute | solution.py:363
  166.0 15.4 %collective-permute-start.7 = (s16[528,256]{1,0:T(8,128)(2,1)S(1)}, s16[528,256]{1,0:T(8,128)(2,1)S(1)}, u32[]{:S(2)}, u32[]{:S(2)}) collective-permute-start(s16[528,256]{1,0:T(8,128)(2,1)S(1)} %chip_sum.1.refs_0_), channel_id=1, source_target_pairs={{0,32},{32,0},{64,96},{96,64},{128,160},{160,128},{192,224},{224,1... | collective-permute-start | bytes 811016 | tf_op jit(solution)/shard_map/ppermute | solution.py:366
  176.3 5.1 %collective-permute-start.10 = (s16[528,256]{1,0:T(8,128)(2,1)S(1)}, s16[528,256]{1,0:T(8,128)(2,1)S(1)}, u32[]{:S(2)}, u32[]{:S(2)}) collective-permute-start(s16[528,256]{1,0:T(8,128)(2,1)S(1)} %collective-permute-done.6.refs_3_), channel_id=1, source_target_pairs={{0,32},{32,0},{64,96},{96,64},{128,160},{160,128},{192,224},{224,1... | collective-permute-start | bytes 811016 | tf_op jit(solution)/shard_map/ppermute | solution.py:366
  177.8 3.6 %collective-permute-start.9 = (s16[528,256]{1,0:T(8,128)(2,1)S(1)}, s16[528,256]{1,0:T(8,128)(2,1)S(1)}, u32[]{:S(2)}, u32[]{:S(2)}) collective-permute-start(s16[528,256]{1,0:T(8,128)(2,1)S(1)} %collective-permute-done.5.refs_2_), channel_id=1, source_target_pairs={{0,32},{32,0},{64,96},{96,64},{128,160},{160,128},{192,224},{224,1... | collective-permute-start | bytes 811016 | tf_op jit(solution)/shard_map/ppermute | solution.py:366
  180.8 1.8 collective-permute-start.8

commit v4 on v3

--- a/solution.py
+++ b/solution.py
@@ -126,9 +126,7 @@
     core = lax.rem(lax.axis_index("replica"), 2)
     half = rows // 2
     for ref, which in ((send_ref, 1 - core), (keep_ref, core)):
-
-        @pl.loop(0, half // LANES)
-        def _(b):
+        for b in range(half // LANES):
             block = which * (half // LANES) + b
             base = pl.multiple_of(block * 2 * LANES, 2 * LANES)
             lo, hi = [
@@ -137,12 +135,11 @@
             ]
             total = jnp.sum(lo * lo + hi * hi, axis=1, keepdims=True)
             ms = jnp.transpose(jnp.broadcast_to(total, (LANES, LANES)))[0:1, :] * (1.0 / (2 * LANES))
-            ms_v[pl.ds(b, 1), :] = ms
+            ms_v[b : b + 1, :] = ms
             coef = -lr / jnp.sqrt(acc_ref[pl.ds(block, 1), :] + ms)
             coef = jnp.transpose(jnp.broadcast_to(coef, (LANES, LANES)))
-            r = pl.multiple_of(b * LANES, LANES)
-            ref[pl.ds(r, LANES), 0:LANES] = lo * coef
-            ref[pl.ds(r, LANES), LANES : 2 * LANES] = hi * coef
+            ref[b * LANES : (b + 1) * LANES, 0:LANES] = lo * coef
+            ref[b * LANES : (b + 1) * LANES, LANES : 2 * LANES] = hi * coef
 
         ref[half : half + half // LANES, 0:LANES] = ms_v[...]
 

time: 189 us -> 182 us (0.963); the launches traced: 187 us -> 182 us
  Pallas kernels: 34.2 us -> 30.1 us
    pallas_call x1, Pallas kernels: 21 us -> 16.9 us  [reduce(): pl.pallas_call(functools.partial(reduce_kernel, cap=cap, rows=rows, lr=lr...]
where the time goes in v4:
time: 182 us
  blocking collectives  110 us (60%)
  Pallas kernels  30.1 us (17%)
  waiting for transfers between devices  27.4 us (15%)
  starting transfers between devices  14.3 us (8%)
    all_to_all x1, blocking collectives, shards(): lax.all_to_all(outgoing, 'mp', split_axis=0, concat_axis=0, tiled=True)  110 us
    ppermute x6, waiting for transfers between devices, hop(): lax.ppermute(v, 'replica', [(k, (k + 2 * chips) % replicas) for k in rang...  22.4 us
    pallas_call x1, Pallas kernels, reduce(): pl.pallas_call(functools.partial(reduce_kernel, cap=cap, rows=rows, lr=lr...  16.9 us
    ppermute x6, starting transfers between devices, hop(): lax.ppermute(v, 'replica', [(k, (k + 2 * chips) % replicas) for k in rang...  8.37 us
    pallas_call x1, Pallas kernels, pack(): pl.pallas_call(functools.partial(pack_kernel, owners=owners, cap=cap, pad...  7.58 us
    ppermute x5, starting transfers between devices, swap(): return lax.ppermute(v, 'replica', [(k, k ^ 1) for k in range(replicas)])  5.96 us
    ppermute x5, waiting for transfers between devices, swap(): return lax.ppermute(v, 'replica', [(k, k ^ 1) for k in range(replicas)])  4.98 us
    pallas_call x1, Pallas kernels, update(): pl.pallas_call(functools.partial(update_kernel, pieces=pieces), out_shape...  3.95 us
  transfers between devices with their start and end apart: 11, of which 6 were waited for; matrix products, arithmetic and copies ran while one was open for 0% of the time, Pallas kernels for 0%

profile of v4, /device:TPU:1, one launch (start us, length us, event | category | flops | bytes accessed | tf_op | source)
XLA Modules:
  0.0 182.3 jit_solution(5477431942555850231)
XLA Ops:
  0.6 7.6 %pack.1 = bf16[32,520,128]{2,1,0:T(8,128)(2,1)S(1)} custom-call(s32[32,128]{1,0:T(8,128)} %bitcast.6, s32[32,128]{1,0:T(8,128)} %bitcast.7, bf16[4096,256]{1,0:T(8,128)(2,1)} %grads_hbm.1), custom_call_target="tpu_custom_call" | custom-call | tf_op jit(solution)/shard_map/pack/pallas_call | solution.py:81
  8.2 0.0 copy-start
  8.2 109.8 %all_to_all.5.recv_ref = bf16[32,520,128]{2,1,0:T(8,128)(2,1)S(1)} all-to-all(bf16[32,520,128]{2,1,0:T(8,128)(2,1)S(1)} %pack.1), channel_id=1, replica_groups=mesh['replica'=8,'mp'=32] {'mp'}, dimensions={0} | all-to-all | bytes 8519680 | tf_op jit(solution)/shard_map/all_to_all | solution.py:356
  118.0 0.0 copy-done
  118.0 16.9 %reduce.1 = (f32[2064,256]{1,0:T(8,128)S(1)}, f32[2064,256]{1,0:T(8,128)S(1)}) custom-call(bf16[32,520,128]{2,1,0:T(8,128)(2,1)S(1)} %all_to_all.5.recv_ref, f32[32,128]{1,0:T(8,128)S(1)} %bitcast.4), custom_call_target="tpu_custom_call" | custom-call | tf_op jit(solution)/shard_map/reduce/pallas_call | solution.py:149
  135.0 2.0 %collective-permute-start = (f32[2064,256]{1,0:T(8,128)S(1)}, f32[2064,256]{1,0:T(8,128)S(1)}, u32[]{:S(2)}, u32[]{:S(2)}) collective-permute-start(f32[2064,256]{1,0:T(8,128)S(1)} %get-tuple-element.11), channel_id=1, source_target_pairs={{0,32},{32,0},{64,96},{96,64},{128,160},{160,128},{192,224},{224,1... | collective-permute-start | bytes 6340616 | tf_op jit(solution)/shard_map/ppermute | solution.py:363
  137.0 3.8 %collective-permute-done.recv_ref = f32[2064,256]{1,0:T(8,128)S(1)} collective-permute-done((f32[2064,256]{1,0:T(8,128)S(1)}, f32[2064,256]{1,0:T(8,128)S(1)}, u32[]{:S(2)}, u32[]{:S(2)}) %collective-permute-start) | collective-permute-done | bytes 2113568 | tf_op jit(solution)/shard_map/ppermute | solution.py:363
  140.8 0.8 pair_sum.1
  141.5 1.5 collective-permute-start.1
  143.1 2.5 %collective-permute-start.2 = (s16[528,256]{1,0:T(8,128)(2,1)S(1)}, s16[528,256]{1,0:T(8,128)(2,1)S(1)}, u32[]{:S(2)}, u32[]{:S(2)}) collective-permute-start(s16[528,256]{1,0:T(8,128)(2,1)S(1)} %get-tuple-element.14), channel_id=1, source_target_pairs={{0,128},{32,160},{64,192},{96,224},{128,0},{160,32},{192,64},{224,... | collective-permute-start | bytes 811016 | tf_op jit(solution)/shard_map/ppermute | solution.py:360
  145.5 1.0 collective-permute-start.3
  146.6 4.0 %collective-permute-done.1.r1 = s16[528,256]{1,0:T(8,128)(2,1)S(1)} collective-permute-done((s16[528,256]{1,0:T(8,128)(2,1)S(1)}, s16[528,256]{1,0:T(8,128)(2,1)S(1)}, u32[]{:S(2)}, u32[]{:S(2)}) %collective-permute-start.1) | collective-permute-done | bytes 270368 | tf_op jit(solution)/shard_map/ppermute | solution.py:360
  150.6 6.9 %collective-permute-done.2.r2 = s16[528,256]{1,0:T(8,128)(2,1)S(1)} collective-permute-done((s16[528,256]{1,0:T(8,128)(2,1)S(1)}, s16[528,256]{1,0:T(8,128)(2,1)S(1)}, u32[]{:S(2)}, u32[]{:S(2)}) %collective-permute-start.2) | collective-permute-done | bytes 270368 | tf_op jit(solution)/shard_map/ppermute | solution.py:360
  157.5 0.0 collective-permute-done.3.r3
  157.5 0.9 chip_sum.1.refs_0_
  158.4 2.7 %collective-permute-start.6 = (s16[528,256]{1,0:T(8,128)(2,1)S(1)}, s16[528,256]{1,0:T(8,128)(2,1)S(1)}, u32[]{:S(2)}, u32[]{:S(2)}) collective-permute-start(s16[528,256]{1,0:T(8,128)(2,1)S(1)} %chip_sum.1.refs_0_), channel_id=1, source_target_pairs={{0,192},{32,224},{64,0},{96,32},{128,64},{160,96},{192,128},{224,1... | collective-permute-start | bytes 811016 | tf_op jit(solution)/shard_map/ppermute | solution.py:360
  161.1 0.2 collective-permute-start.5
  161.3 0.5 collective-permute-start.4
  161.7 1.9 %collective-permute-start.7 = (s16[528,256]{1,0:T(8,128)(2,1)S(1)}, s16[528,256]{1,0:T(8,128)(2,1)S(1)}, u32[]{:S(2)}, u32[]{:S(2)}) collective-permute-start(s16[528,256]{1,0:T(8,128)(2,1)S(1)} %chip_sum.1.refs_0_), channel_id=1, source_target_pairs={{0,32},{32,0},{64,96},{96,64},{128,160},{160,128},{192,224},{224,1... | collective-permute-start | bytes 811016 | tf_op jit(solution)/shard_map/ppermute | solution.py:363
  163.6 8.4 %collective-permute-done.6.refs_3_ = s16[528,256]{1,0:T(8,128)(2,1)S(1)} collective-permute-done((s16[528,256]{1,0:T(8,128)(2,1)S(1)}, s16[528,256]{1,0:T(8,128)(2,1)S(1)}, u32[]{:S(2)}, u32[]{:S(2)}) %collective-permute-start.6) | collective-permute-done | bytes 270368 | tf_op jit(solution)/shard_map/ppermute | solution.py:360
  172.1 1.5 collective-permute-start.10
  173.6 0.0 collective-permute-done.5.refs_2_
  173.6 0.0 collective-permute-start.9
  173.6 3.0 %collective-permute-done.4.refs_1_ = s16[528,256]{1,0:T(8,128)(2,1)S(1)} collective-permute-done((s16[528,256]{1,0:T(8,128)(2,1)S(1)}, s16[528,256]{1,0:T(8,128)(2,1)S(1)}, u32[]{:S(2)}, u32[]{:S(2)}) %collective-permute-start.4) | collective-permute-done | bytes 270368 | tf_op jit(solution)/shard_map/ppermute | solution.py:360
  176.6 0.6 collective-permute-start.8
  177.2 0.0 collective-permute-done.7.refs_4_
  177.2 0.0 collective-permute-done.10.refs_7_
  177.2 0.0 collective-permute-done.9.refs_6_
  177.2 1.2 collective-permute-done.8.refs_5_
  178.3 4.0 %update.1 = (f32[4096,256]{1,0:T(8,128)}, f32[32,128]{1,0:T(8,128)}) custom-call(f32[4096,256]{1,0:T(8,128)} %emb_hbm.1, f32[32,128]{1,0:T(8,128)S(1)} %bitcast.5, s16[528,256]{1,0:T(8,128)(2,1)S(1)} %chip_sum.1.refs_0_, s16[528,256]{1,0:T(8,128)(2,1)S(1)} %collective-permute-done.4.refs_1_, s16[528,256]{1,0:T(8,128)(2,1)S(1)} %collective-permute-done.5.refs_2_, ...), custom_call_target="tpu_custom_call" | custom-call | tf_op jit(solution)/shard_map/update/pallas_call | solution.py:327
Async XLA Ops:
  8.2 109.8 %copy-start = (f32[4096]{0:T(1024)S(1)}, f32[4096]{0:T(1024)}, u32[]{:S(2)}) copy-start(f32[4096]{0:T(1024)} %param.6) | copy-start | bytes 49156
  135.0 5.8 %collective-permute-start = (f32[2064,256]{1,0:T(8,128)S(1)}, f32[2064,256]{1,0:T(8,128)S(1)}, u32[]{:S(2)}, u32[]{:S(2)}) collective-permute-start(f32[2064,256]{1,0:T(8,128)S(1)} %get-tuple-element.11), channel_id=1, source_target_pairs={{0,32},{32,0},{64,96},{96,64},{128,160},{160,128},{192,224},{224,1... | collective-permute-start | bytes 6340616 | tf_op jit(solution)/shard_map/ppermute | solution.py:363
  141.5 9.0 %collective-permute-start.1 = (s16[528,256]{1,0:T(8,128)(2,1)S(1)}, s16[528,256]{1,0:T(8,128)(2,1)S(1)}, u32[]{:S(2)}, u32[]{:S(2)}) collective-permute-start(s16[528,256]{1,0:T(8,128)(2,1)S(1)} %get-tuple-element.13), channel_id=1, source_target_pairs={{0,64},{32,96},{64,128},{96,160},{128,192},{160,224},{192,0},{224,... | collective-permute-start | bytes 811016 | tf_op jit(solution)/shard_map/ppermute | solution.py:360
  143.1 14.4 %collective-permute-start.2 = (s16[528,256]{1,0:T(8,128)(2,1)S(1)}, s16[528,256]{1,0:T(8,128)(2,1)S(1)}, u32[]{:S(2)}, u32[]{:S(2)}) collective-permute-start(s16[528,256]{1,0:T(8,128)(2,1)S(1)} %get-tuple-element.14), channel_id=1, source_target_pairs={{0,128},{32,160},{64,192},{96,224},{128,0},{160,32},{192,64},{224,... | collective-permute-start | bytes 811016 | tf_op jit(solution)/shard_map/ppermute | solution.py:360
  145.5 12.0 %collective-permute-start.3 = (s16[528,256]{1,0:T(8,128)(2,1)S(1)}, s16[528,256]{1,0:T(8,128)(2,1)S(1)}, u32[]{:S(2)}, u32[]{:S(2)}) collective-permute-start(s16[528,256]{1,0:T(8,128)(2,1)S(1)} %get-tuple-element.15), channel_id=1, source_target_pairs={{0,192},{32,224},{64,0},{96,32},{128,64},{160,96},{192,128},{224,1... | collective-permute-start | bytes 811016 | tf_op jit(solution)/shard_map/ppermute | solution.py:360
  158.4 13.7 %collective-permute-start.6 = (s16[528,256]{1,0:T(8,128)(2,1)S(1)}, s16[528,256]{1,0:T(8,128)(2,1)S(1)}, u32[]{:S(2)}, u32[]{:S(2)}) collective-permute-start(s16[528,256]{1,0:T(8,128)(2,1)S(1)} %chip_sum.1.refs_0_), channel_id=1, source_target_pairs={{0,192},{32,224},{64,0},{96,32},{128,64},{160,96},{192,128},{224,1... | collective-permute-start | bytes 811016 | tf_op jit(solution)/shard_map/ppermute | solution.py:360
  161.1 12.5 %collective-permute-start.5 = (s16[528,256]{1,0:T(8,128)(2,1)S(1)}, s16[528,256]{1,0:T(8,128)(2,1)S(1)}, u32[]{:S(2)}, u32[]{:S(2)}) collective-permute-start(s16[528,256]{1,0:T(8,128)(2,1)S(1)} %chip_sum.1.refs_0_), channel_id=1, source_target_pairs={{0,128},{32,160},{64,192},{96,224},{128,0},{160,32},{192,64},{224,... | collective-permute-start | bytes 811016 | tf_op jit(solution)/shard_map/ppermute | solution.py:360
  161.3 15.3 %collective-permute-start.4 = (s16[528,256]{1,0:T(8,128)(2,1)S(1)}, s16[528,256]{1,0:T(8,128)(2,1)S(1)}, u32[]{:S(2)}, u32[]{:S(2)}) collective-permute-start(s16[528,256]{1,0:T(8,128)(2,1)S(1)} %chip_sum.1.refs_0_), channel_id=1, source_target_pairs={{0,64},{32,96},{64,128},{96,160},{128,192},{160,224},{192,0},{224,... | collective-permute-start | bytes 811016 | tf_op jit(solution)/shard_map/ppermute | solution.py:360
  161.7 15.4 %collective-permute-start.7 = (s16[528,256]{1,0:T(8,128)(2,1)S(1)}, s16[528,256]{1,0:T(8,128)(2,1)S(1)}, u32[]{:S(2)}, u32[]{:S(2)}) collective-permute-start(s16[528,256]{1,0:T(8,128)(2,1)S(1)} %chip_sum.1.refs_0_), channel_id=1, source_target_pairs={{0,32},{32,0},{64,96},{96,64},{128,160},{160,128},{192,224},{224,1... | collective-permute-start | bytes 811016 | tf_op jit(solution)/shard_map/ppermute | solution.py:363
  172.1 5.1 %collective-permute-start.10 = (s16[528,256]{1,0:T(8,128)(2,1)S(1)}, s16[528,256]{1,0:T(8,128)(2,1)S(1)}, u32[]{:S(2)}, u32[]{:S(2)}) collective-permute-start(s16[528,256]{1,0:T(8,128)(2,1)S(1)} %collective-permute-done.6.refs_3_), channel_id=1, source_target_pairs={{0,32},{32,0},{64,96},{96,64},{128,160},{160,128},{192,224},{224,1... | collective-permute-start | bytes 811016 | tf_op jit(solution)/shard_map/ppermute | solution.py:363
  173.6 3.6 %collective-permute-start.9 = (s16[528,256]{1,0:T(8,128)(2,1)S(1)}, s16[528,256]{1,0:T(8,128)(2,1)S(1)}, u32[]{:S(2)}, u32[]{:S(2)}) collective-permute-start(s16[528,256]{1,0:T(8,128)(2,1)S(1)} %collective-permute-done.5.refs_2_), channel_id=1, source_target_pairs={{0,32},{32,0},{64,96},{96,64},{128,160},{160,128},{192,224},{224,1... | collective-permute-start | bytes 811016 | tf_op jit(solution)/shard_map/ppermute | solution.py:363
  176.6 1.8 collective-permute-start.8

commit v5 on v4

--- a/solution.py
+++ b/solution.py
@@ -98,8 +98,8 @@
     )(*[pltpu.with_memory_space_constraint(x, pltpu.HBM) for x in (owner, row, grads)])
 
 
-def reduce_kernel(recv_ref, acc_ref, keep_ref, send_ref, xbuf, a0, a1, a2, a3, ms_v, idx_v, idx_s, sem, *, cap, rows, lr):
-    accs = [a0, a1, a2, a3]
+def reduce_kernel(recv_ref, acc_ref, keep_ref, send_ref, xbuf, a0, a1, a2, a3, a4, a5, ms_v, idx_v, idx_s, sem, *, cap, rows, lr):
+    accs = [a0, a1, a2, a3, a4, a5]
     owners = recv_ref.shape[0]
     @pl.loop(0, owners)
     def _(o):
@@ -121,7 +121,7 @@
         for h in range(2):
             for j in range(LANES):
                 at = pl.ds(idx_s[2 * o + h, j], 2)
-                accs[j % 4][at, :] += xbuf[2 * (h * LANES + j) : 2 * (h * LANES + j) + 2, :]
+                accs[j % 6][at, :] += xbuf[2 * (h * LANES + j) : 2 * (h * LANES + j) + 2, :]
 
     core = lax.rem(lax.axis_index("replica"), 2)
     half = rows // 2
@@ -130,7 +130,7 @@
             block = which * (half // LANES) + b
             base = pl.multiple_of(block * 2 * LANES, 2 * LANES)
             lo, hi = [
-                (a0[at, :] + a1[at, :]) + (a2[at, :] + a3[at, :])
+                ((a0[at, :] + a1[at, :]) + (a2[at, :] + a3[at, :])) + (a4[at, :] + a5[at, :])
                 for at in (pl.ds(base, LANES, stride=2), pl.ds(base + 1, LANES, stride=2))
             ]
             total = jnp.sum(lo * lo + hi * hi, axis=1, keepdims=True)
@@ -152,14 +152,14 @@
         in_specs=[pl.BlockSpec(memory_space=pltpu.VMEM)] * 2,
         out_specs=(pl.BlockSpec(memory_space=pltpu.VMEM), pl.BlockSpec(memory_space=pltpu.VMEM)),
         scratch_shapes=[pltpu.VMEM((2 * cap, LANES), jnp.float32)]
-        + [pltpu.VMEM((2 * rows + 8, LANES), jnp.float32)] * 4
+        + [pltpu.VMEM((2 * rows + 8, LANES), jnp.float32)] * 6
         + [
             pltpu.VMEM((rows // 2 // LANES, LANES), jnp.float32),
             pltpu.VMEM((2 * recv.shape[0], LANES), jnp.int32),
             pltpu.SMEM((2 * recv.shape[0], LANES), jnp.int32),
             pltpu.SemaphoreType.DMA,
         ],
-        compiler_params=pltpu.CompilerParams(vmem_limit_bytes=32 << 20),
+        compiler_params=pltpu.CompilerParams(vmem_limit_bytes=42 << 20),
         name="reduce",
     )(recv, acc2d)
 

time: 182 us -> 179 us (0.984)
  Pallas kernels: 30.1 us -> 27.4 us
    pallas_call x1, Pallas kernels: 16.9 us -> 14.3 us  [reduce(): pl.pallas_call(functools.partial(reduce_kernel, cap=cap, rows=rows, lr=lr...]
where the time goes in v5:
time: 179 us; the launch traced here: 180 us
  blocking collectives  110 us (61%)
  Pallas kernels  27.4 us (15%)
  waiting for transfers between devices  27.1 us (15%)
  starting transfers between devices  14.6 us (8%)
    all_to_all x1, blocking collectives, shards(): lax.all_to_all(outgoing, 'mp', split_axis=0, concat_axis=0, tiled=True)  110 us
    ppermute x6, waiting for transfers between devices, hop(): lax.ppermute(v, 'replica', [(k, (k + 2 * chips) % replicas) for k in rang...  22.1 us
    pallas_call x1, Pallas kernels, reduce(): pl.pallas_call(functools.partial(reduce_kernel, cap=cap, rows=rows, lr=lr...  14.3 us
    ppermute x6, starting transfers between devices, hop(): lax.ppermute(v, 'replica', [(k, (k + 2 * chips) % replicas) for k in rang...  8.34 us
    pallas_call x1, Pallas kernels, pack(): pl.pallas_call(functools.partial(pack_kernel, owners=owners, cap=cap, pad...  7.58 us
    ppermute x5, starting transfers between devices, swap(): return lax.ppermute(v, 'replica', [(k, k ^ 1) for k in range(replicas)])  6.26 us
    ppermute x5, waiting for transfers between devices, swap(): return lax.ppermute(v, 'replica', [(k, k ^ 1) for k in range(replicas)])  4.98 us
    pallas_call x1, Pallas kernels, update(): pl.pallas_call(functools.partial(update_kernel, pieces=pieces), out_shape...  3.95 us
  transfers between devices with their start and end apart: 11, of which 6 were waited for; matrix products, arithmetic and copies ran while one was open for 0% of the time, Pallas kernels for 0%

profile of v5, /device:TPU:1, one launch (start us, length us, event | category | flops | bytes accessed | tf_op | source)
XLA Modules:
  0.0 179.6 jit_solution(14196118496103240683)
XLA Ops:
  0.6 7.6 %pack.1 = bf16[32,520,128]{2,1,0:T(8,128)(2,1)S(1)} custom-call(s32[32,128]{1,0:T(8,128)} %bitcast.6, s32[32,128]{1,0:T(8,128)} %bitcast.7, bf16[4096,256]{1,0:T(8,128)(2,1)} %grads_hbm.1), custom_call_target="tpu_custom_call" | custom-call | tf_op jit(solution)/shard_map/pack/pallas_call | solution.py:81
  8.2 0.0 copy-start
  8.2 109.8 %all_to_all.5.recv_ref = bf16[32,520,128]{2,1,0:T(8,128)(2,1)S(1)} all-to-all(bf16[32,520,128]{2,1,0:T(8,128)(2,1)S(1)} %pack.1), channel_id=1, replica_groups=mesh['replica'=8,'mp'=32] {'mp'}, dimensions={0} | all-to-all | bytes 8519680 | tf_op jit(solution)/shard_map/all_to_all | solution.py:356
  118.0 0.0 copy-done
  118.0 14.3 %reduce.1 = (f32[2064,256]{1,0:T(8,128)S(1)}, f32[2064,256]{1,0:T(8,128)S(1)}) custom-call(bf16[32,520,128]{2,1,0:T(8,128)(2,1)S(1)} %all_to_all.5.recv_ref, f32[32,128]{1,0:T(8,128)S(1)} %bitcast.4), custom_call_target="tpu_custom_call" | custom-call | tf_op jit(solution)/shard_map/reduce/pallas_call | solution.py:149
  132.3 2.1 %collective-permute-start = (f32[2064,256]{1,0:T(8,128)S(1)}, f32[2064,256]{1,0:T(8,128)S(1)}, u32[]{:S(2)}, u32[]{:S(2)}) collective-permute-start(f32[2064,256]{1,0:T(8,128)S(1)} %get-tuple-element.11), channel_id=1, source_target_pairs={{0,32},{32,0},{64,96},{96,64},{128,160},{160,128},{192,224},{224,1... | collective-permute-start | bytes 6340616 | tf_op jit(solution)/shard_map/ppermute | solution.py:363
  134.4 3.8 %collective-permute-done.recv_ref = f32[2064,256]{1,0:T(8,128)S(1)} collective-permute-done((f32[2064,256]{1,0:T(8,128)S(1)}, f32[2064,256]{1,0:T(8,128)S(1)}, u32[]{:S(2)}, u32[]{:S(2)}) %collective-permute-start) | collective-permute-done | bytes 2113568 | tf_op jit(solution)/shard_map/ppermute | solution.py:363
  138.3 0.8 pair_sum.1
  139.0 1.3 collective-permute-start.1
  140.3 2.5 %collective-permute-start.2 = (s16[528,256]{1,0:T(8,128)(2,1)S(1)}, s16[528,256]{1,0:T(8,128)(2,1)S(1)}, u32[]{:S(2)}, u32[]{:S(2)}) collective-permute-start(s16[528,256]{1,0:T(8,128)(2,1)S(1)} %get-tuple-element.14), channel_id=1, source_target_pairs={{0,128},{32,160},{64,192},{96,224},{128,0},{160,32},{192,64},{224,... | collective-permute-start | bytes 811016 | tf_op jit(solution)/shard_map/ppermute | solution.py:360
  142.8 1.1 collective-permute-start.3
  144.0 4.0 %collective-permute-done.1.r1 = s16[528,256]{1,0:T(8,128)(2,1)S(1)} collective-permute-done((s16[528,256]{1,0:T(8,128)(2,1)S(1)}, s16[528,256]{1,0:T(8,128)(2,1)S(1)}, u32[]{:S(2)}, u32[]{:S(2)}) %collective-permute-start.1) | collective-permute-done | bytes 270368 | tf_op jit(solution)/shard_map/ppermute | solution.py:360
  148.0 6.8 %collective-permute-done.2.r2 = s16[528,256]{1,0:T(8,128)(2,1)S(1)} collective-permute-done((s16[528,256]{1,0:T(8,128)(2,1)S(1)}, s16[528,256]{1,0:T(8,128)(2,1)S(1)}, u32[]{:S(2)}, u32[]{:S(2)}) %collective-permute-start.2) | collective-permute-done | bytes 270368 | tf_op jit(solution)/shard_map/ppermute | solution.py:360
  154.8 0.0 collective-permute-done.3.r3
  154.8 0.9 chip_sum.1.refs_0_
  155.7 2.7 %collective-permute-start.6 = (s16[528,256]{1,0:T(8,128)(2,1)S(1)}, s16[528,256]{1,0:T(8,128)(2,1)S(1)}, u32[]{:S(2)}, u32[]{:S(2)}) collective-permute-start(s16[528,256]{1,0:T(8,128)(2,1)S(1)} %chip_sum.1.refs_0_), channel_id=1, source_target_pairs={{0,192},{32,224},{64,0},{96,32},{128,64},{160,96},{192,128},{224,1... | collective-permute-start | bytes 811016 | tf_op jit(solution)/shard_map/ppermute | solution.py:360
  158.4 0.1 collective-permute-start.5
  158.6 0.5 collective-permute-start.4
  159.1 2.0 %collective-permute-start.7 = (s16[528,256]{1,0:T(8,128)(2,1)S(1)}, s16[528,256]{1,0:T(8,128)(2,1)S(1)}, u32[]{:S(2)}, u32[]{:S(2)}) collective-permute-start(s16[528,256]{1,0:T(8,128)(2,1)S(1)} %chip_sum.1.refs_0_), channel_id=1, source_target_pairs={{0,32},{32,0},{64,96},{96,64},{128,160},{160,128},{192,224},{224,1... | collective-permute-start | bytes 811016 | tf_op jit(solution)/shard_map/ppermute | solution.py:363
  161.1 8.3 %collective-permute-done.6.refs_3_ = s16[528,256]{1,0:T(8,128)(2,1)S(1)} collective-permute-done((s16[528,256]{1,0:T(8,128)(2,1)S(1)}, s16[528,256]{1,0:T(8,128)(2,1)S(1)}, u32[]{:S(2)}, u32[]{:S(2)}) %collective-permute-start.6) | collective-permute-done | bytes 270368 | tf_op jit(solution)/shard_map/ppermute | solution.py:360
  169.4 1.5 collective-permute-start.10
  170.9 0.0 collective-permute-done.5.refs_2_
  170.9 0.0 collective-permute-start.9
  170.9 2.9 %collective-permute-done.4.refs_1_ = s16[528,256]{1,0:T(8,128)(2,1)S(1)} collective-permute-done((s16[528,256]{1,0:T(8,128)(2,1)S(1)}, s16[528,256]{1,0:T(8,128)(2,1)S(1)}, u32[]{:S(2)}, u32[]{:S(2)}) %collective-permute-start.4) | collective-permute-done | bytes 270368 | tf_op jit(solution)/shard_map/ppermute | solution.py:360
  173.8 0.7 collective-permute-start.8
  174.5 0.0 collective-permute-done.7.refs_4_
  174.5 0.0 collective-permute-done.10.refs_7_
  174.5 0.0 collective-permute-done.9.refs_6_
  174.5 1.2 collective-permute-done.8.refs_5_
  175.6 4.0 %update.1 = (f32[4096,256]{1,0:T(8,128)}, f32[32,128]{1,0:T(8,128)}) custom-call(f32[4096,256]{1,0:T(8,128)} %emb_hbm.1, f32[32,128]{1,0:T(8,128)S(1)} %bitcast.5, s16[528,256]{1,0:T(8,128)(2,1)S(1)} %chip_sum.1.refs_0_, s16[528,256]{1,0:T(8,128)(2,1)S(1)} %collective-permute-done.4.refs_1_, s16[528,256]{1,0:T(8,128)(2,1)S(1)} %collective-permute-done.5.refs_2_, ...), custom_call_target="tpu_custom_call" | custom-call | tf_op jit(solution)/shard_map/update/pallas_call | solution.py:327
Async XLA Ops:
  8.2 109.8 %copy-start = (f32[4096]{0:T(1024)S(1)}, f32[4096]{0:T(1024)}, u32[]{:S(2)}) copy-start(f32[4096]{0:T(1024)} %param.6) | copy-start | bytes 49156
  132.3 5.9 %collective-permute-start = (f32[2064,256]{1,0:T(8,128)S(1)}, f32[2064,256]{1,0:T(8,128)S(1)}, u32[]{:S(2)}, u32[]{:S(2)}) collective-permute-start(f32[2064,256]{1,0:T(8,128)S(1)} %get-tuple-element.11), channel_id=1, source_target_pairs={{0,32},{32,0},{64,96},{96,64},{128,160},{160,128},{192,224},{224,1... | collective-permute-start | bytes 6340616 | tf_op jit(solution)/shard_map/ppermute | solution.py:363
  139.0 8.9 %collective-permute-start.1 = (s16[528,256]{1,0:T(8,128)(2,1)S(1)}, s16[528,256]{1,0:T(8,128)(2,1)S(1)}, u32[]{:S(2)}, u32[]{:S(2)}) collective-permute-start(s16[528,256]{1,0:T(8,128)(2,1)S(1)} %get-tuple-element.13), channel_id=1, source_target_pairs={{0,64},{32,96},{64,128},{96,160},{128,192},{160,224},{192,0},{224,... | collective-permute-start | bytes 811016 | tf_op jit(solution)/shard_map/ppermute | solution.py:360
  140.3 14.5 %collective-permute-start.2 = (s16[528,256]{1,0:T(8,128)(2,1)S(1)}, s16[528,256]{1,0:T(8,128)(2,1)S(1)}, u32[]{:S(2)}, u32[]{:S(2)}) collective-permute-start(s16[528,256]{1,0:T(8,128)(2,1)S(1)} %get-tuple-element.14), channel_id=1, source_target_pairs={{0,128},{32,160},{64,192},{96,224},{128,0},{160,32},{192,64},{224,... | collective-permute-start | bytes 811016 | tf_op jit(solution)/shard_map/ppermute | solution.py:360
  142.8 12.0 %collective-permute-start.3 = (s16[528,256]{1,0:T(8,128)(2,1)S(1)}, s16[528,256]{1,0:T(8,128)(2,1)S(1)}, u32[]{:S(2)}, u32[]{:S(2)}) collective-permute-start(s16[528,256]{1,0:T(8,128)(2,1)S(1)} %get-tuple-element.15), channel_id=1, source_target_pairs={{0,192},{32,224},{64,0},{96,32},{128,64},{160,96},{192,128},{224,1... | collective-permute-start | bytes 811016 | tf_op jit(solution)/shard_map/ppermute | solution.py:360
  155.7 13.7 %collective-permute-start.6 = (s16[528,256]{1,0:T(8,128)(2,1)S(1)}, s16[528,256]{1,0:T(8,128)(2,1)S(1)}, u32[]{:S(2)}, u32[]{:S(2)}) collective-permute-start(s16[528,256]{1,0:T(8,128)(2,1)S(1)} %chip_sum.1.refs_0_), channel_id=1, source_target_pairs={{0,192},{32,224},{64,0},{96,32},{128,64},{160,96},{192,128},{224,1... | collective-permute-start | bytes 811016 | tf_op jit(solution)/shard_map/ppermute | solution.py:360
  158.4 12.5 %collective-permute-start.5 = (s16[528,256]{1,0:T(8,128)(2,1)S(1)}, s16[528,256]{1,0:T(8,128)(2,1)S(1)}, u32[]{:S(2)}, u32[]{:S(2)}) collective-permute-start(s16[528,256]{1,0:T(8,128)(2,1)S(1)} %chip_sum.1.refs_0_), channel_id=1, source_target_pairs={{0,128},{32,160},{64,192},{96,224},{128,0},{160,32},{192,64},{224,... | collective-permute-start | bytes 811016 | tf_op jit(solution)/shard_map/ppermute | solution.py:360
  158.6 15.2 %collective-permute-start.4 = (s16[528,256]{1,0:T(8,128)(2,1)S(1)}, s16[528,256]{1,0:T(8,128)(2,1)S(1)}, u32[]{:S(2)}, u32[]{:S(2)}) collective-permute-start(s16[528,256]{1,0:T(8,128)(2,1)S(1)} %chip_sum.1.refs_0_), channel_id=1, source_target_pairs={{0,64},{32,96},{64,128},{96,160},{128,192},{160,224},{192,0},{224,... | collective-permute-start | bytes 811016 | tf_op jit(solution)/shard_map/ppermute | solution.py:360
  159.1 15.4 %collective-permute-start.7 = (s16[528,256]{1,0:T(8,128)(2,1)S(1)}, s16[528,256]{1,0:T(8,128)(2,1)S(1)}, u32[]{:S(2)}, u32[]{:S(2)}) collective-permute-start(s16[528,256]{1,0:T(8,128)(2,1)S(1)} %chip_sum.1.refs_0_), channel_id=1, source_target_pairs={{0,32},{32,0},{64,96},{96,64},{128,160},{160,128},{192,224},{224,1... | collective-permute-start | bytes 811016 | tf_op jit(solution)/shard_map/ppermute | solution.py:363
  169.4 5.0 %collective-permute-start.10 = (s16[528,256]{1,0:T(8,128)(2,1)S(1)}, s16[528,256]{1,0:T(8,128)(2,1)S(1)}, u32[]{:S(2)}, u32[]{:S(2)}) collective-permute-start(s16[528,256]{1,0:T(8,128)(2,1)S(1)} %collective-permute-done.6.refs_3_), channel_id=1, source_target_pairs={{0,32},{32,0},{64,96},{96,64},{128,160},{160,128},{192,224},{224,1... | collective-permute-start | bytes 811016 | tf_op jit(solution)/shard_map/ppermute | solution.py:363
  170.9 3.5 %collective-permute-start.9 = (s16[528,256]{1,0:T(8,128)(2,1)S(1)}, s16[528,256]{1,0:T(8,128)(2,1)S(1)}, u32[]{:S(2)}, u32[]{:S(2)}) collective-permute-start(s16[528,256]{1,0:T(8,128)(2,1)S(1)} %collective-permute-done.5.refs_2_), channel_id=1, source_target_pairs={{0,32},{32,0},{64,96},{96,64},{128,160},{160,128},{192,224},{224,1... | collective-permute-start | bytes 811016 | tf_op jit(solution)/shard_map/ppermute | solution.py:363
  173.8 1.8 %collective-permute-start.8 = (s16[528,256]{1,0:T(8,128)(2,1)S(1)}, s16[528,256]{1,0:T(8,128)(2,1)S(1)}, u32[]{:S(2)}, u32[]{:S(2)}) collective-permute-start(s16[528,256]{1,0:T(8,128)(2,1)S(1)} %collective-permute-done.4.refs_1_), channel_id=1, source_target_pairs={{0,32},{32,0},{64,96},{96,64},{128,160},{160,128},{192,224},{224,1... | collective-permute-start | bytes 811016 | tf_op jit(solution)/shard_map/ppermute | solution.py:363

commit v6 on v5

--- a/solution.py
+++ b/solution.py
@@ -291,8 +291,8 @@
     )(own, r1, r2, r3)
 
 
-def update_kernel(emb_hbm, acc_ref, *refs, pieces):
-    codes, (table_hbm, accum_ref, buf, tail, in_sems, out_sems) = refs[:pieces], refs[pieces:]
+def update_kernel(emb_ref, acc_ref, *refs, pieces):
+    codes, (table_hbm, accum_ref, buf, tail, out_sems) = refs[:pieces], refs[pieces:]
     part = buf.shape[1]
     blocks = part // LANES
     me = lax.axis_index("replica")
@@ -302,18 +302,15 @@
         for k in range(pieces)
     ]
     spans = [pl.ds(pl.multiple_of(place * part, part), part) for place in places]
-    loads = [pltpu.make_async_copy(emb_hbm.at[span], buf.at[k], in_sems.at[k]) for k, span in enumerate(spans)]
     stores = [pltpu.make_async_copy(buf.at[k], table_hbm.at[span], out_sems.at[k]) for k, span in enumerate(spans)]
-    for load in loads:
-        load.start()
     for k, ref in enumerate(codes):
         tail[...] = from_i16(ref[part : part + 16, :])
-        loads[k].wait()
         for j in range(blocks):
             lo, hi, ms = decode(ref, tail, j)
             rows = slice(j * LANES, (j + 1) * LANES)
-            buf[k, rows, 0:LANES] += lo
-            buf[k, rows, LANES : 2 * LANES] += hi
+            from_row = pl.ds(pl.multiple_of(places[k] * part + j * LANES, LANES), LANES)
+            buf[k, rows, 0:LANES] = emb_ref[from_row, 0:LANES] + lo
+            buf[k, rows, LANES : 2 * LANES] = emb_ref[from_row, LANES : 2 * LANES] + hi
             at = pl.ds(places[k] * blocks + j, 1)
             accum_ref[at, :] = acc_ref[at, :] + ms
         stores[k].start()
@@ -327,17 +324,16 @@
     return pl.pallas_call(
         functools.partial(update_kernel, pieces=pieces),
         out_shape=(jax.ShapeDtypeStruct(emb.shape, jnp.float32), jax.ShapeDtypeStruct(acc2d.shape, jnp.float32)),
-        in_specs=[pl.BlockSpec(memory_space=pltpu.HBM)] + [pl.BlockSpec(memory_space=pltpu.VMEM)] * (1 + pieces),
+        in_specs=[pl.BlockSpec(memory_space=pltpu.VMEM)] * (2 + pieces),
         out_specs=(pl.BlockSpec(memory_space=pltpu.HBM), pl.BlockSpec(memory_space=pltpu.VMEM)),
         scratch_shapes=[
             pltpu.VMEM((pieces, part, 2 * LANES), jnp.float32),
             pltpu.VMEM((16, 2 * LANES), jnp.float32),
             pltpu.SemaphoreType.DMA((pieces,)),
-            pltpu.SemaphoreType.DMA((pieces,)),
         ],
         compiler_params=pltpu.CompilerParams(vmem_limit_bytes=20 << 20),
         name="update",
-    )(pltpu.with_memory_space_constraint(emb, pltpu.HBM), acc2d, *codes)
+    )(emb, acc2d, *codes)
 
 
 learn_rate = 0.5

time: 179 us -> 179 us (level)
  no operation moved by 1% of the time
where the time goes in v6:
time: 179 us
  blocking collectives  110 us (61%)
  waiting for transfers between devices  27.3 us (15%)
  Pallas kernels  26.3 us (15%)
  starting transfers between devices  14.5 us (8%)
    all_to_all x1, blocking collectives, shards(): lax.all_to_all(outgoing, 'mp', split_axis=0, concat_axis=0, tiled=True)  110 us
    ppermute x6, waiting for transfers between devices, hop(): lax.ppermute(v, 'replica', [(k, (k + 2 * chips) % replicas) for k in rang...  22.3 us
    pallas_call x1, Pallas kernels, reduce(): pl.pallas_call(functools.partial(reduce_kernel, cap=cap, rows=rows, lr=lr...  14.2 us
    ppermute x6, starting transfers between devices, hop(): lax.ppermute(v, 'replica', [(k, (k + 2 * chips) % replicas) for k in rang...  8.32 us
    pallas_call x1, Pallas kernels, pack(): pl.pallas_call(functools.partial(pack_kernel, owners=owners, cap=cap, pad...  7.58 us
    ppermute x5, starting transfers between devices, swap(): return lax.ppermute(v, 'replica', [(k, k ^ 1) for k in range(replicas)])  6.19 us
    ppermute x5, waiting for transfers between devices, swap(): return lax.ppermute(v, 'replica', [(k, k ^ 1) for k in range(replicas)])  4.98 us
  transfers between devices with their start and end apart: 11, of which 6 were waited for; matrix products, arithmetic and copies ran while one was open for 0% of the time, Pallas kernels for 0%

profile of v6, /device:TPU:1, one launch (start us, length us, event | category | flops | bytes accessed | tf_op | source)
XLA Modules:
  0.0 178.5 jit_solution(13624637265889305884)
XLA Ops:
  0.6 7.6 %pack.1 = bf16[32,520,128]{2,1,0:T(8,128)(2,1)S(1)} custom-call(s32[32,128]{1,0:T(8,128)} %bitcast.6, s32[32,128]{1,0:T(8,128)} %bitcast.7, bf16[4096,256]{1,0:T(8,128)(2,1)} %grads_hbm.1), custom_call_target="tpu_custom_call" | custom-call | tf_op jit(solution)/shard_map/pack/pallas_call | solution.py:81
  8.2 0.0 copy-start.1
  8.2 109.8 %all_to_all.5.recv_ref = bf16[32,520,128]{2,1,0:T(8,128)(2,1)S(1)} all-to-all(bf16[32,520,128]{2,1,0:T(8,128)(2,1)S(1)} %pack.1), channel_id=1, replica_groups=mesh['replica'=8,'mp'=32] {'mp'}, dimensions={0} | all-to-all | bytes 8519680 | tf_op jit(solution)/shard_map/all_to_all | solution.py:352
  118.0 0.0 copy-done.1
  118.0 0.0 copy-start
  118.0 14.2 %reduce.1 = (f32[2064,256]{1,0:T(8,128)S(1)}, f32[2064,256]{1,0:T(8,128)S(1)}) custom-call(bf16[32,520,128]{2,1,0:T(8,128)(2,1)S(1)} %all_to_all.5.recv_ref, f32[32,128]{1,0:T(8,128)S(1)} %bitcast.4), custom_call_target="tpu_custom_call" | custom-call | tf_op jit(solution)/shard_map/reduce/pallas_call | solution.py:149
  132.3 2.2 %collective-permute-start = (f32[2064,256]{1,0:T(8,128)S(1)}, f32[2064,256]{1,0:T(8,128)S(1)}, u32[]{:S(2)}, u32[]{:S(2)}) collective-permute-start(f32[2064,256]{1,0:T(8,128)S(1)} %get-tuple-element.11), channel_id=1, source_target_pairs={{0,32},{32,0},{64,96},{96,64},{128,160},{160,128},{192,224},{224,1... | collective-permute-start | bytes 6340616 | tf_op jit(solution)/shard_map/ppermute | solution.py:359
  134.5 3.8 %collective-permute-done.recv_ref = f32[2064,256]{1,0:T(8,128)S(1)} collective-permute-done((f32[2064,256]{1,0:T(8,128)S(1)}, f32[2064,256]{1,0:T(8,128)S(1)}, u32[]{:S(2)}, u32[]{:S(2)}) %collective-permute-start) | collective-permute-done | bytes 2113568 | tf_op jit(solution)/shard_map/ppermute | solution.py:359
  138.3 0.8 pair_sum.1
  139.0 1.3 collective-permute-start.1
  140.4 2.4 %collective-permute-start.2 = (s16[528,256]{1,0:T(8,128)(2,1)S(1)}, s16[528,256]{1,0:T(8,128)(2,1)S(1)}, u32[]{:S(2)}, u32[]{:S(2)}) collective-permute-start(s16[528,256]{1,0:T(8,128)(2,1)S(1)} %get-tuple-element.14), channel_id=1, source_target_pairs={{0,128},{32,160},{64,192},{96,224},{128,0},{160,32},{192,64},{224,... | collective-permute-start | bytes 811016 | tf_op jit(solution)/shard_map/ppermute | solution.py:356
  142.8 1.1 collective-permute-start.3
  143.9 4.1 %collective-permute-done.1.r1 = s16[528,256]{1,0:T(8,128)(2,1)S(1)} collective-permute-done((s16[528,256]{1,0:T(8,128)(2,1)S(1)}, s16[528,256]{1,0:T(8,128)(2,1)S(1)}, u32[]{:S(2)}, u32[]{:S(2)}) %collective-permute-start.1) | collective-permute-done | bytes 270368 | tf_op jit(solution)/shard_map/ppermute | solution.py:356
  148.0 6.8 %collective-permute-done.2.r2 = s16[528,256]{1,0:T(8,128)(2,1)S(1)} collective-permute-done((s16[528,256]{1,0:T(8,128)(2,1)S(1)}, s16[528,256]{1,0:T(8,128)(2,1)S(1)}, u32[]{:S(2)}, u32[]{:S(2)}) %collective-permute-start.2) | collective-permute-done | bytes 270368 | tf_op jit(solution)/shard_map/ppermute | solution.py:356
  154.8 0.0 collective-permute-done.3.r3
  154.8 0.9 chip_sum.1.refs_0_
  155.7 2.8 %collective-permute-start.6 = (s16[528,256]{1,0:T(8,128)(2,1)S(1)}, s16[528,256]{1,0:T(8,128)(2,1)S(1)}, u32[]{:S(2)}, u32[]{:S(2)}) collective-permute-start(s16[528,256]{1,0:T(8,128)(2,1)S(1)} %chip_sum.1.refs_0_), channel_id=1, source_target_pairs={{0,192},{32,224},{64,0},{96,32},{128,64},{160,96},{192,128},{224,1... | collective-permute-start | bytes 811016 | tf_op jit(solution)/shard_map/ppermute | solution.py:356
  158.4 0.2 collective-permute-start.5
  158.6 0.5 collective-permute-start.4
  159.1 1.9 %collective-permute-start.7 = (s16[528,256]{1,0:T(8,128)(2,1)S(1)}, s16[528,256]{1,0:T(8,128)(2,1)S(1)}, u32[]{:S(2)}, u32[]{:S(2)}) collective-permute-start(s16[528,256]{1,0:T(8,128)(2,1)S(1)} %chip_sum.1.refs_0_), channel_id=1, source_target_pairs={{0,32},{32,0},{64,96},{96,64},{128,160},{160,128},{192,224},{224,1... | collective-permute-start | bytes 811016 | tf_op jit(solution)/shard_map/ppermute | solution.py:359
  161.0 8.4 %collective-permute-done.6.refs_3_ = s16[528,256]{1,0:T(8,128)(2,1)S(1)} collective-permute-done((s16[528,256]{1,0:T(8,128)(2,1)S(1)}, s16[528,256]{1,0:T(8,128)(2,1)S(1)}, u32[]{:S(2)}, u32[]{:S(2)}) %collective-permute-start.6) | collective-permute-done | bytes 270368 | tf_op jit(solution)/shard_map/ppermute | solution.py:356
  169.4 1.5 collective-permute-start.10
  170.9 0.0 collective-permute-done.5.refs_2_
  170.9 0.0 collective-permute-start.9
  170.9 3.0 %collective-permute-done.4.refs_1_ = s16[528,256]{1,0:T(8,128)(2,1)S(1)} collective-permute-done((s16[528,256]{1,0:T(8,128)(2,1)S(1)}, s16[528,256]{1,0:T(8,128)(2,1)S(1)}, u32[]{:S(2)}, u32[]{:S(2)}) %collective-permute-start.4) | collective-permute-done | bytes 270368 | tf_op jit(solution)/shard_map/ppermute | solution.py:356
  173.9 0.6 collective-permute-start.8
  174.5 0.0 collective-permute-done.7.refs_4_
  174.5 0.0 collective-permute-done.10.refs_7_
  174.5 0.0 collective-permute-done.9.refs_6_
  174.5 1.2 collective-permute-done.8.refs_5_
  175.7 0.0 copy-done
  175.7 2.8 %update.1 = (f32[4096,256]{1,0:T(8,128)}, f32[32,128]{1,0:T(8,128)}) custom-call(f32[4096,256]{1,0:T(8,128)S(1)} %copy-done, f32[32,128]{1,0:T(8,128)S(1)} %bitcast.5, s16[528,256]{1,0:T(8,128)(2,1)S(1)} %chip_sum.1.refs_0_, s16[528,256]{1,0:T(8,128)(2,1)S(1)} %collective-permute-done.4.refs_1_, s16[528,256]{1,0:T(8,128)(2,1)S(1)} %collective-permute-done.5.refs_2_, ...), custom_call_target="tpu_custom_call" | custom-call | tf_op jit(solution)/shard_map/update/pallas_call | solution.py:324
Async XLA Ops:
  8.2 109.8 %copy-start.1 = (f32[4096]{0:T(1024)S(1)}, f32[4096]{0:T(1024)}, u32[]{:S(2)}) copy-start(f32[4096]{0:T(1024)} %param.6) | copy-start | bytes 49156
  118.0 57.7 %copy-start = (f32[4096,256]{1,0:T(8,128)S(1)}, f32[4096,256]{1,0:T(8,128)}, u32[]{:S(2)}) copy-start(f32[4096,256]{1,0:T(8,128)} %emb_ref.1) | copy-start | bytes 12582916
  132.3 6.0 %collective-permute-start = (f32[2064,256]{1,0:T(8,128)S(1)}, f32[2064,256]{1,0:T(8,128)S(1)}, u32[]{:S(2)}, u32[]{:S(2)}) collective-permute-start(f32[2064,256]{1,0:T(8,128)S(1)} %get-tuple-element.11), channel_id=1, source_target_pairs={{0,32},{32,0},{64,96},{96,64},{128,160},{160,128},{192,224},{224,1... | collective-permute-start | bytes 6340616 | tf_op jit(solution)/shard_map/ppermute | solution.py:359
  139.0 8.9 %collective-permute-start.1 = (s16[528,256]{1,0:T(8,128)(2,1)S(1)}, s16[528,256]{1,0:T(8,128)(2,1)S(1)}, u32[]{:S(2)}, u32[]{:S(2)}) collective-permute-start(s16[528,256]{1,0:T(8,128)(2,1)S(1)} %get-tuple-element.13), channel_id=1, source_target_pairs={{0,64},{32,96},{64,128},{96,160},{128,192},{160,224},{192,0},{224,... | collective-permute-start | bytes 811016 | tf_op jit(solution)/shard_map/ppermute | solution.py:356
  140.4 14.4 %collective-permute-start.2 = (s16[528,256]{1,0:T(8,128)(2,1)S(1)}, s16[528,256]{1,0:T(8,128)(2,1)S(1)}, u32[]{:S(2)}, u32[]{:S(2)}) collective-permute-start(s16[528,256]{1,0:T(8,128)(2,1)S(1)} %get-tuple-element.14), channel_id=1, source_target_pairs={{0,128},{32,160},{64,192},{96,224},{128,0},{160,32},{192,64},{224,... | collective-permute-start | bytes 811016 | tf_op jit(solution)/shard_map/ppermute | solution.py:356
  142.8 12.0 %collective-permute-start.3 = (s16[528,256]{1,0:T(8,128)(2,1)S(1)}, s16[528,256]{1,0:T(8,128)(2,1)S(1)}, u32[]{:S(2)}, u32[]{:S(2)}) collective-permute-start(s16[528,256]{1,0:T(8,128)(2,1)S(1)} %get-tuple-element.15), channel_id=1, source_target_pairs={{0,192},{32,224},{64,0},{96,32},{128,64},{160,96},{192,128},{224,1... | collective-permute-start | bytes 811016 | tf_op jit(solution)/shard_map/ppermute | solution.py:356
  155.7 13.8 %collective-permute-start.6 = (s16[528,256]{1,0:T(8,128)(2,1)S(1)}, s16[528,256]{1,0:T(8,128)(2,1)S(1)}, u32[]{:S(2)}, u32[]{:S(2)}) collective-permute-start(s16[528,256]{1,0:T(8,128)(2,1)S(1)} %chip_sum.1.refs_0_), channel_id=1, source_target_pairs={{0,192},{32,224},{64,0},{96,32},{128,64},{160,96},{192,128},{224,1... | collective-permute-start | bytes 811016 | tf_op jit(solution)/shard_map/ppermute | solution.py:356
  158.4 12.5 %collective-permute-start.5 = (s16[528,256]{1,0:T(8,128)(2,1)S(1)}, s16[528,256]{1,0:T(8,128)(2,1)S(1)}, u32[]{:S(2)}, u32[]{:S(2)}) collective-permute-start(s16[528,256]{1,0:T(8,128)(2,1)S(1)} %chip_sum.1.refs_0_), channel_id=1, source_target_pairs={{0,128},{32,160},{64,192},{96,224},{128,0},{160,32},{192,64},{224,... | collective-permute-start | bytes 811016 | tf_op jit(solution)/shard_map/ppermute | solution.py:356
  158.6 15.3 %collective-permute-start.4 = (s16[528,256]{1,0:T(8,128)(2,1)S(1)}, s16[528,256]{1,0:T(8,128)(2,1)S(1)}, u32[]{:S(2)}, u32[]{:S(2)}) collective-permute-start(s16[528,256]{1,0:T(8,128)(2,1)S(1)} %chip_sum.1.refs_0_), channel_id=1, source_target_pairs={{0,64},{32,96},{64,128},{96,160},{128,192},{160,224},{192,0},{224,... | collective-permute-start | bytes 811016 | tf_op jit(solution)/shard_map/ppermute | solution.py:356
  159.1 15.4 %collective-permute-start.7 = (s16[528,256]{1,0:T(8,128)(2,1)S(1)}, s16[528,256]{1,0:T(8,128)(2,1)S(1)}, u32[]{:S(2)}, u32[]{:S(2)}) collective-permute-start(s16[528,256]{1,0:T(8,128)(2,1)S(1)} %chip_sum.1.refs_0_), channel_id=1, source_target_pairs={{0,32},{32,0},{64,96},{96,64},{128,160},{160,128},{192,224},{224,1... | collective-permute-start | bytes 811016 | tf_op jit(solution)/shard_map/ppermute | solution.py:359
  169.4 5.1 %collective-permute-start.10 = (s16[528,256]{1,0:T(8,128)(2,1)S(1)}, s16[528,256]{1,0:T(8,128)(2,1)S(1)}, u32[]{:S(2)}, u32[]{:S(2)}) collective-permute-start(s16[528,256]{1,0:T(8,128)(2,1)S(1)} %collective-permute-done.6.refs_3_), channel_id=1, source_target_pairs={{0,32},{32,0},{64,96},{96,64},{128,160},{160,128},{192,224},{224,1... | collective-permute-start | bytes 811016 | tf_op jit(solution)/shard_map/ppermute | solution.py:359
  170.9 3.6 %collective-permute-start.9 = (s16[528,256]{1,0:T(8,128)(2,1)S(1)}, s16[528,256]{1,0:T(8,128)(2,1)S(1)}, u32[]{:S(2)}, u32[]{:S(2)}) collective-permute-start(s16[528,256]{1,0:T(8,128)(2,1)S(1)} %collective-permute-done.5.refs_2_), channel_id=1, source_target_pairs={{0,32},{32,0},{64,96},{96,64},{128,160},{160,128},{192,224},{224,1... | collective-permute-start | bytes 811016 | tf_op jit(solution)/shard_map/ppermute | solution.py:359
  173.9 1.8 collective-permute-start.8
